TPU v7x, 32 devices: a whole 2x2x4 slice. The times are simulated.
32 devices in a mesh: section: 2 (over x), dp: 4 (over z), row: 2 (over y), col: 2 (over core).
Axes of the slice: x: 2, y: 2, z: 4, core: 2. Of those that a mesh axis runs over, the one named last changes fastest.
Arguments:
- latents_in: bfloat16 [4096, 384], P(('dp', 'row'), 'col'), may hold values from -4 to 4
- labels: int32 [16], P(('dp', 'row')), may hold values from 0 to 999
- timesteps: int32 [16], P(('dp', 'row')), may hold values from 0 to 999
- out_grad: bfloat16 [4096, 384], P(('dp', 'row'), 'col'), may hold values from -6 to 6
- label_table: bfloat16 [1000, 384], replicated, may hold values from -6 to 6
- time_table: bfloat16 [1000, 384], replicated, may hold values from -6 to 6
- ada_w: bfloat16 [2, 384, 6, 384], P('section', None, None, 'col'), may hold values from -0.3125 to 0.3125
- ada_b: float32 [2, 6, 384], P('section', None, 'col'), may hold values from -1.5 to 1.5
- qkv_w: bfloat16 [2, 384, 3, 384], P('section', 'col', None, 'row'), may hold values from -0.3125 to 0.3125
- qkv_b: float32 [2, 3, 384], P('section', None, 'row'), may hold values from -1.5 to 1.5
- proj_w: bfloat16 [2, 384, 384], P('section', 'row', 'col'), may hold values from -2.5 to 2.5
- proj_b: float32 [2, 384], P('section', 'col'), may hold values from -1.5 to 1.5
- fc1_w: bfloat16 [2, 384, 1536], P('section', 'col', 'row'), may hold values from -0.3125 to 0.3125
- fc1_b: float32 [2, 1536], P('section', 'row'), may hold values from -1.5 to 1.5
- fc2_w: bfloat16 [2, 1536, 384], P('section', 'row', 'col'), may hold values from -0.15625 to 0.15625
- fc2_b: float32 [2, 384], P('section', 'col'), may hold values from -1.5 to 1.5
Outputs:
- block_outs: bfloat16 [2, 4096, 384], P('section', ('dp', 'row'), 'col')
- input_grads: float32 [2, 4096, 384], P('section', ('dp', 'row'), 'col')
- cond_grad: float32 [16, 384], P(('dp', 'row'))
- label_table_grad: float32 [1000, 384], replicated
- time_table_grad: float32 [1000, 384], replicated
- ada_w_grad: float32 [2, 384, 6, 384], P('section', None, None, 'col')
- ada_b_grad: float32 [2, 6, 384], P('section', None, 'col')
- qkv_w_grad: float32 [2, 384, 3, 384], P('section', 'col', None, 'row')
- qkv_b_grad: float32 [2, 3, 384], P('section', None, 'row')
- proj_w_grad: float32 [2, 384, 384], P('section', 'row', 'col')
- proj_b_grad: float32 [2, 384], P('section', 'col')
- fc1_w_grad: float32 [2, 384, 1536], P('section', 'col', 'row')
- fc1_b_grad: float32 [2, 1536], P('section', 'row')
- fc2_w_grad: float32 [2, 1536, 384], P('section', 'row', 'col')
- fc2_b_grad: float32 [2, 384], P('section', 'col')
All inputs are finite; a program needn't handle non-finite values.
Results may differ from a plain program's by a relative error of at most 0.035.
The roundings to bfloat16 on the way count: a program that leaves them out, or rounds other values in their place, can miss the bound.
Values may be sent and summed in bfloat16 or wider, within the bound.
A program may use at most 128 MiB of HBM per device.

v0:
```python
import math

import jax
import jax.numpy as jnp
from jax import lax
from jax.sharding import PartitionSpec as P

D = 384
HD = 64
SEQ = 256
MICRO = 2


EPS = 1e-06


def shifted(block, axis, distance):
    devices = range(lax.axis_size(axis))
    route = [(i - distance, i) for i in devices if i - distance in devices]
    return lax.ppermute(block, axis, route)


def as_sent(shard):
    return jax.tree.map(lambda a: a.astype(jnp.bfloat16) if a.dtype == jnp.float32 else a, shard)


def rows_gather(value):
    return lax.all_gather(value, "row", axis=0, tiled=True)


def cols_gather(value):
    return lax.all_gather(value, "col", axis=0, tiled=True)


def rows_total(value):
    return lax.psum_scatter(value, "row", scatter_dimension=0, tiled=True)


def cols_total(value):
    return lax.psum_scatter(value, "col", scatter_dimension=0, tiled=True)


def feature_sums(first, second):
    return lax.psum((first, second), "col")


def matmul(left_arr, right_arr):
    return jnp.dot(left_arr, right_arr, preferred_element_type=jnp.float32)


def matmul_left_t(left_arr, right_arr):
    return jnp.einsum("ta,tb->ab", left_arr, right_arr, preferred_element_type=jnp.float32)


def matmul_right_t(left_arr, right_arr):
    return jnp.einsum("tb,ab->ta", left_arr, right_arr, preferred_element_type=jnp.float32)


def norm_rows(stream):
    row_sums, squares = feature_sums(jnp.sum(stream, axis=-1), jnp.sum(stream * stream, axis=-1))
    mean_val = row_sums / D
    variance = squares / D - mean_val * mean_val
    inv_std = lax.rsqrt(variance + EPS)
    return ((stream - mean_val[:, None]) * inv_std[:, None], inv_std)


def norm_back(grad_norm, normed, inv_std):
    first_sum, second_sum = feature_sums(
        jnp.sum(grad_norm, axis=-1), jnp.sum(grad_norm * normed, axis=-1)
    )
    return inv_std[:, None] * (
        grad_norm - first_sum[:, None] / D - normed * (second_sum[:, None] / D)
    )


def gelu_back(pre_act, grad_act):
    return jax.vjp(lambda value: jax.nn.gelu(value, approximate=True), pre_act)[1](grad_act)[0]


def latent_sum(values):
    return jnp.sum(values.reshape(-1, SEQ, values.shape[-1]), axis=1)


def token_mods(chosen):
    return [
        jnp.broadcast_to(
            chosen[:, index_mod][:, None, :], (chosen.shape[0], SEQ, chosen.shape[2])
        ).reshape(-1, chosen.shape[2])
        for index_mod in range(6)
    ]


def split_heads(packed, head_count):
    parts = packed.reshape(-1, SEQ, 3, head_count, HD)
    return (parts[:, :, 0], parts[:, :, 1], parts[:, :, 2])


def attend(packed, head_count):
    queries, keys_part, values = split_heads(packed, head_count)
    scores = jnp.einsum(
        "lqhd,lkhd->lhqk", queries, keys_part, preferred_element_type=jnp.float32
    ) * (1.0 / math.sqrt(HD))
    log_total = jax.nn.logsumexp(scores, axis=-1)
    prob_low = jnp.exp(scores - log_total[..., None]).astype(jnp.bfloat16)
    attended = jnp.einsum("lhqk,lkhd->lqhd", prob_low, values, preferred_element_type=jnp.float32)
    return (attended.astype(jnp.bfloat16).reshape(-1, head_count * HD), log_total)


def attend_back(packed, log_total, grad_att, head_count):
    queries, keys_part, values = split_heads(packed, head_count)
    scale = 1.0 / math.sqrt(HD)
    scores = (
        jnp.einsum("lqhd,lkhd->lhqk", queries, keys_part, preferred_element_type=jnp.float32)
        * scale
    )
    prob_full = jnp.exp(scores - log_total[..., None])
    prob_low = prob_full.astype(jnp.bfloat16)
    grad_heads = grad_att.reshape(-1, SEQ, head_count, HD)
    grad_values = jnp.einsum(
        "lhqk,lqhd->lkhd", prob_low, grad_heads, preferred_element_type=jnp.float32
    )
    grad_prob = jnp.einsum(
        "lqhd,lkhd->lhqk", grad_heads, values, preferred_element_type=jnp.float32
    )
    delta = jnp.sum(prob_full * grad_prob, axis=-1, keepdims=True)
    grad_scores = (prob_full * (grad_prob - delta) * scale).astype(jnp.bfloat16)
    grad_queries = jnp.einsum(
        "lhqk,lkhd->lqhd", grad_scores, keys_part, preferred_element_type=jnp.float32
    )
    grad_keys = jnp.einsum(
        "lhqk,lqhd->lkhd", grad_scores, queries, preferred_element_type=jnp.float32
    )
    stacked = jnp.stack([grad_queries, grad_keys, grad_values], axis=2).astype(jnp.bfloat16)
    return stacked.reshape(-1, 3 * head_count * HD)


def block_forward(stream_low, modul, params):
    w_qkv, b_qkv, w_proj, b_proj, w_up, b_up, w_down, b_down = params
    head_count = w_proj.shape[0] // HD
    stream = stream_low.astype(jnp.float32)
    normed1, inv1 = norm_rows(stream)
    hidden1_all = rows_gather((normed1 * (1.0 + modul[1]) + modul[0]).astype(jnp.bfloat16))
    packed = (cols_total(matmul(hidden1_all, w_qkv)) + b_qkv).astype(jnp.bfloat16)
    attended, log_total = attend(packed, head_count)
    attended_all = cols_gather(attended)
    branch_a = rows_total(matmul(attended_all, w_proj)) + b_proj
    middle = stream + modul[2] * branch_a
    normed2, inv2 = norm_rows(middle)
    hidden2_all = rows_gather((normed2 * (1.0 + modul[4]) + modul[3]).astype(jnp.bfloat16))
    pre_act = cols_total(matmul(hidden2_all, w_up)) + b_up
    activ_all = cols_gather(jax.nn.gelu(pre_act, approximate=True).astype(jnp.bfloat16))
    branch_f = rows_total(matmul(activ_all, w_down)) + b_down
    result = (middle + modul[5] * branch_f).astype(jnp.bfloat16)
    saved = (
        normed1,
        inv1,
        hidden1_all,
        packed,
        log_total,
        attended_all,
        branch_a,
        normed2,
        inv2,
        hidden2_all,
        pre_act,
        activ_all,
        branch_f,
    )
    return (result, saved)


def block_backward(grad_out, modul, params, saved):
    w_qkv, b_qkv, w_proj, b_proj, w_up, b_up, w_down, b_down = params
    (
        normed1,
        inv1,
        hidden1_all,
        packed,
        log_total,
        attended_all,
        branch_a,
        normed2,
        inv2,
        hidden2_all,
        pre_act,
        activ_all,
        branch_f,
    ) = saved
    head_count = w_proj.shape[0] // HD
    d_gate2 = latent_sum(grad_out * branch_f)
    grad_f = rows_gather((grad_out * modul[5]).astype(jnp.bfloat16))
    g_down = matmul_left_t(activ_all, grad_f)
    g_bdown = jnp.sum(grad_f, axis=0, dtype=jnp.float32)
    grad_act = cols_total(matmul_right_t(grad_f, w_down))
    grad_pre = cols_gather(gelu_back(pre_act, grad_act).astype(jnp.bfloat16))
    g_up = matmul_left_t(hidden2_all, grad_pre)
    g_bup = jnp.sum(grad_pre, axis=0, dtype=jnp.float32)
    grad_h2 = rows_total(matmul_right_t(grad_pre, w_up))
    d_scale2 = latent_sum(grad_h2 * normed2)
    d_shift2 = latent_sum(grad_h2)
    grad_mid = grad_out + norm_back(grad_h2 * (1.0 + modul[4]), normed2, inv2)
    d_gate1 = latent_sum(grad_mid * branch_a)
    grad_a = rows_gather((grad_mid * modul[2]).astype(jnp.bfloat16))
    g_proj = matmul_left_t(attended_all, grad_a)
    g_bproj = jnp.sum(grad_a, axis=0, dtype=jnp.float32)
    grad_att = cols_total(matmul_right_t(grad_a, w_proj)).astype(jnp.bfloat16)
    grad_packed = cols_gather(attend_back(packed, log_total, grad_att, head_count))
    g_qkv = matmul_left_t(hidden1_all, grad_packed)
    g_bqkv = jnp.sum(grad_packed, axis=0, dtype=jnp.float32)
    grad_h1 = rows_total(matmul_right_t(grad_packed, w_qkv))
    d_scale1 = latent_sum(grad_h1 * normed1)
    d_shift1 = latent_sum(grad_h1)
    grad_in = grad_mid + norm_back(grad_h1 * (1.0 + modul[1]), normed1, inv1)
    d_mod = jnp.stack([d_shift1, d_scale1, d_gate1, d_shift2, d_scale2, d_gate2], axis=1)
    return (grad_in, (g_qkv, g_bqkv, g_proj, g_bproj, g_up, g_bup, g_down, g_bdown), d_mod)


def on_device(
    latents_in,
    labels,
    timesteps,
    out_grad,
    label_table,
    time_table,
    ada_w,
    ada_b,
    qkv_w,
    qkv_b,
    proj_w,
    proj_b,
    fc1_w,
    fc1_b,
    fc2_w,
    fc2_b,
):
    section_zero = lax.axis_index("section") == 0
    col_width = latents_in.shape[1]
    row_width = qkv_w.shape[3]
    mb_tokens = latents_in.shape[0] // MICRO
    mb_latents = mb_tokens // SEQ
    class_ids = jnp.arange(label_table.shape[0], dtype=jnp.int32)
    step_ids = jnp.arange(time_table.shape[0], dtype=jnp.int32)
    label_hot = (labels[:, None] == class_ids[None, :]).astype(jnp.bfloat16)
    time_hot = (timesteps[:, None] == step_ids[None, :]).astype(jnp.bfloat16)
    cond = matmul(label_hot, label_table) + matmul(time_hot, time_table)
    silu_low = jax.nn.silu(cond).astype(jnp.bfloat16)
    ada_flat = ada_w[0].reshape(D, 6 * col_width)
    params = (
        qkv_w[0].reshape(col_width, 3 * row_width),
        qkv_b[0].reshape(3 * row_width),
        proj_w[0],
        proj_b[0],
        fc1_w[0],
        fc1_b[0],
        fc2_w[0],
        fc2_b[0],
    )
    modul_all = (matmul(silu_low, ada_flat) + ada_b[0].reshape(6 * col_width)).reshape(
        -1, 6, col_width
    )
    stream_width = latents_in.shape[1]
    shapes = [leaf.shape for leaf in params]

    def latent_block(source, micro_index):
        return source[micro_index * mb_latents : (micro_index + 1) * mb_latents]

    def pick_section(left_arr, right_arr):
        return jnp.where(section_zero, left_arr, right_arr)

    received = jnp.zeros((mb_tokens, stream_width), jnp.bfloat16)
    forward_outs = []
    forward_saves = []
    for tick_index in range(MICRO + 1):
        current_mb = min(tick_index, MICRO - 1)
        prior_mb = max(tick_index - 1, 0)
        own_block = latents_in[current_mb * mb_tokens : (current_mb + 1) * mb_tokens]
        inputs = pick_section(own_block, received)
        chosen = pick_section(
            latent_block(modul_all, current_mb), latent_block(modul_all, prior_mb)
        )
        result, saved = block_forward(inputs, token_mods(chosen), params)
        forward_outs.append(result)
        forward_saves.append(saved)
        if tick_index < MICRO:
            received = shifted(result, "section", 1)
    grad_in = jnp.zeros((mb_tokens, stream_width), jnp.float32)
    totals = tuple((jnp.zeros(shape, jnp.float32) for shape in shapes))
    grad_list = []
    dmod_list = []
    for tick_index in range(MICRO + 1):
        current_mb = min(tick_index, MICRO - 1)
        prior_mb = max(tick_index - 1, 0)
        saved = jax.tree.map(pick_section, forward_saves[prior_mb], forward_saves[current_mb + 1])
        chosen = pick_section(
            latent_block(modul_all, prior_mb), latent_block(modul_all, current_mb)
        )
        cotangent = out_grad[current_mb * mb_tokens : (current_mb + 1) * mb_tokens].astype(
            jnp.float32
        )
        grad_out = pick_section(grad_in, cotangent)
        is_valid = pick_section(jnp.asarray(tick_index >= 1), jnp.asarray(tick_index < MICRO))
        grad_x, grads, d_mod = block_backward(grad_out, token_mods(chosen), params, saved)
        totals = tuple(
            (
                left_arr + jnp.where(is_valid, right_arr, 0.0)
                for left_arr, right_arr in zip(totals, grads)
            )
        )
        grad_list.append(grad_x)
        dmod_list.append(d_mod)
        if tick_index < MICRO:
            grad_in = shifted(grad_x.astype(jnp.bfloat16), "section", -1).astype(grad_x.dtype)
    block_outs = jnp.concatenate(
        [
            pick_section(forward_outs[micro_index], forward_outs[micro_index + 1])
            for micro_index in range(MICRO)
        ],
        axis=0,
    )
    input_grads = jnp.concatenate(
        [
            pick_section(grad_list[micro_index + 1], grad_list[micro_index])
            for micro_index in range(MICRO)
        ],
        axis=0,
    )
    dmod_all = jnp.concatenate(
        [
            pick_section(dmod_list[micro_index + 1], dmod_list[micro_index])
            for micro_index in range(MICRO)
        ],
        axis=0,
    )
    reduced = jax.tree.map(lambda part: part.astype(jnp.float32), lax.psum(as_sent(totals), "dp"))
    dmod_flat = dmod_all.reshape(-1, 6 * col_width)
    dmod_low = dmod_flat.astype(jnp.bfloat16)
    cond_pull = lax.psum(matmul_right_t(dmod_low, ada_flat), ("section", "col"))
    cond_grad = jax.vjp(jax.nn.silu, cond)[1](cond_pull)[0]
    latent_ids = jnp.stack([labels, timesteps], axis=1).astype(jnp.float32)
    class_float = class_ids.astype(jnp.float32)
    step_float = step_ids.astype(jnp.float32)
    grad_piece = lax.all_gather(cond_grad, ("dp", "row"), axis=0, tiled=True)
    dmod_piece = lax.all_gather(dmod_flat, ("dp", "row"), axis=0, tiled=True)
    silu_piece = lax.all_gather(silu_low.astype(jnp.float32), ("dp", "row"), axis=0, tiled=True)
    id_piece = lax.all_gather(latent_ids, ("dp", "row"), axis=0, tiled=True)
    ada_sum = matmul_left_t(silu_piece.astype(jnp.bfloat16), dmod_piece.astype(jnp.bfloat16))
    adab_sum = jnp.sum(dmod_piece, axis=0)
    label_rows = (id_piece[:, 0:1] == class_float[None, :]).astype(jnp.float32)
    step_rows = (id_piece[:, 1:2] == step_float[None, :]).astype(jnp.float32)
    label_sum = jnp.einsum("nc,na->ca", label_rows, grad_piece, precision=lax.Precision.HIGHEST)
    time_sum = jnp.einsum("nc,na->ca", step_rows, grad_piece, precision=lax.Precision.HIGHEST)
    return (
        block_outs[None],
        input_grads[None],
        cond_grad,
        label_sum,
        time_sum,
        ada_sum.reshape(D, 6, col_width)[None],
        adab_sum.reshape(6, col_width)[None],
        reduced[0].reshape(col_width, 3, row_width)[None],
        reduced[1].reshape(3, row_width)[None],
        reduced[2][None],
        reduced[3][None],
        reduced[4][None],
        reduced[5][None],
        reduced[6][None],
        reduced[7][None],
    )


def solution(mesh):
    return jax.shard_map(
        on_device,
        mesh=mesh,
        in_specs=(
            P(("dp", "row"), "col"),
            P(("dp", "row")),
            P(("dp", "row")),
            P(("dp", "row"), "col"),
            P(),
            P(),
            P("section", None, None, "col"),
            P("section", None, "col"),
            P("section", "col", None, "row"),
            P("section", None, "row"),
            P("section", "row", "col"),
            P("section", "col"),
            P("section", "col", "row"),
            P("section", "row"),
            P("section", "row", "col"),
            P("section", "col"),
        ),
        out_specs=(
            P("section", ("dp", "row"), "col"),
            P("section", ("dp", "row"), "col"),
            P(("dp", "row"), None),
            P(),
            P(),
            P("section", None, None, "col"),
            P("section", None, "col"),
            P("section", "col", None, "row"),
            P("section", None, "row"),
            P("section", "row", "col"),
            P("section", "col"),
            P("section", "col", "row"),
            P("section", "row"),
            P("section", "row", "col"),
            P("section", "col"),
        ),
        check_vma=False,
    )
```

profile of v0, /device:TPU:0, one launch (start us, length us, event | category | flops | bytes accessed | tf_op | source)
XLA Modules:
  0.0 635.9 jit_solution(6507734537738554974)
XLA Ops:
  14.4 6.6 %all_gather.84 = bf16[512,192]{0,1:T(8,128)(2,1)S(1)} all-gather(bf16[256,192]{0,1:T(8,128)(2,1)S(1)} %fusion.148), channel_id=1, replica_groups=mesh['section'=2,'dp'=4,'row'=2,'col'=2] {'row'}, dimensions={0}, use_global_device_ids=true | all-gather | bytes 294912 | tf_op jit(solution)/shard_map/all_gather | solution.py:28
  22.7 9.9 %reduce-scatter.25.cloned.1.call-done = f32[256,576]{0,1:T(8,128)} async-done(((f32[512,576]{0,1:T(8,128)}), f32[256,576]{0,1:T(8,128)}) %reduce-scatter.25.cloned.1.call-update) | async-done | bytes 589840 | tf_op jit(solution)/shard_map/reduce_scatter | solution.py:40
  37.6 14.5 %reduce-scatter.27.cloned.1.call-done = f32[256,192]{0,1:T(8,128)} async-done(((f32[512,192]{0,1:T(8,128)}), f32[256,192]{0,1:T(8,128)}) %reduce-scatter.27.cloned.1.call-update) | async-done | bytes 196624 | tf_op jit(solution)/shard_map/reduce_scatter | solution.py:36
  63.1 9.1 %reduce-scatter.29.cloned.1.call-done = f32[256,768]{1,0:T(8,128)} async-done(((f32[512,768]{1,0:T(8,128)}), f32[256,768]{1,0:T(8,128)}) %reduce-scatter.29.cloned.1.call-update) | async-done | bytes 786448 | tf_op jit(solution)/shard_map/reduce_scatter | solution.py:40
  77.4 14.5 %reduce-scatter.31.cloned.1.call-done = f32[256,192]{0,1:T(8,128)} async-done(((f32[512,192]{0,1:T(8,128)}), f32[256,192]{0,1:T(8,128)}) %reduce-scatter.31.cloned.1.call-update) | async-done | bytes 196624 | tf_op jit(solution)/shard_map/reduce_scatter | solution.py:36
  102.4 5.7 all_gather.88
  109.5 9.5 %reduce-scatter.33.cloned.1.call-done = f32[256,576]{0,1:T(8,128)} async-done(((f32[512,576]{0,1:T(8,128)}), f32[256,576]{0,1:T(8,128)}) %reduce-scatter.33.cloned.1.call-update) | async-done | bytes 589840 | tf_op jit(solution)/shard_map/reduce_scatter | solution.py:40
  125.3 5.9 all_gather.96
  132.9 6.9 %reduce-scatter.35.cloned.1.call-done = f32[256,192]{0,1:T(8,128)} async-done(((f32[512,192]{0,1:T(8,128)}), f32[256,192]{0,1:T(8,128)}) %reduce-scatter.35.cloned.1.call-update) | async-done | bytes 196624 | tf_op jit(solution)/shard_map/reduce_scatter | solution.py:36
  152.4 11.9 %reduce-scatter.37.cloned.1.call-done = f32[256,768]{1,0:T(8,128)} async-done(((f32[512,768]{1,0:T(8,128)}), f32[256,768]{1,0:T(8,128)}) %reduce-scatter.37.cloned.1.call-update) | async-done | bytes 786448 | tf_op jit(solution)/shard_map/reduce_scatter | solution.py:40
  174.7 10.8 %reduce-scatter.39.cloned.1.call-done = f32[256,192]{0,1:T(8,128)} async-done(((f32[512,192]{0,1:T(8,128)}), f32[256,192]{0,1:T(8,128)}) %reduce-scatter.39.cloned.1.call-update) | async-done | bytes 196624 | tf_op jit(solution)/shard_map/reduce_scatter | solution.py:36
  191.3 10.0 %reduce-scatter.51.cloned.1.call-done = f32[256,192]{0,1:T(8,128)} async-done(((f32[512,192]{0,1:T(8,128)}), f32[256,192]{0,1:T(8,128)}) %reduce-scatter.51.cloned.1.call-update) | async-done | bytes 196624 | tf_op jit(solution)/shard_map/reduce_scatter | solution.py:36
  251.3 6.0 reduce-scatter.55.cloned.1.call-done
  259.0 14.1 %reduce-scatter.43.cloned.1.call-done = f32[256,192]{0,1:T(8,128)} async-done(((f32[512,192]{0,1:T(8,128)}), f32[256,192]{0,1:T(8,128)}) %reduce-scatter.43.cloned.1.call-update) | async-done | bytes 196624 | tf_op jit(solution)/shard_map/reduce_scatter | solution.py:36
  280.6 5.5 all_gather.94
  307.5 8.2 %reduce-scatter.57.cloned.1.call-done = f32[256,768]{1,0:T(8,128)} async-done(((f32[512,768]{1,0:T(8,128)}), f32[256,768]{1,0:T(8,128)}) %reduce-scatter.57.cloned.1.call-update) | async-done | bytes 786448 | tf_op jit(solution)/shard_map/reduce_scatter | solution.py:40
  323.5 13.4 %reduce-scatter.59.cloned.1.call-done = f32[256,192]{0,1:T(8,128)} async-done(((f32[512,192]{0,1:T(8,128)}), f32[256,192]{0,1:T(8,128)}) %reduce-scatter.59.cloned.1.call-update) | async-done | bytes 196624 | tf_op jit(solution)/shard_map/reduce_scatter | solution.py:36
  380.5 21.0 %all-gather = f32[8,2,2]{2,1,0:T(2,128)S(1)} all-gather(f32[1,2,2]{2,1,0:T(2,128)} %bitcast.418), channel_id=1, replica_groups=mesh['section'=2,'dp'=4,'row'=2,'col'=2] {'dp','row'}, dimensions={0}, use_global_device_ids=true | all-gather | bytes 144 | tf_op jit(solution)/shard_map/all_gather | solution.py:345
  468.6 7.7 %all_gather.106 = bf16[512,192]{0,1:T(8,128)(2,1)S(1)} all-gather(bf16[256,192]{0,1:T(8,128)(2,1)S(1)} %multiply_convert_fusion), channel_id=1, replica_groups=mesh['section'=2,'dp'=4,'row'=2,'col'=2] {'row'}, dimensions={0}, use_global_device_ids=true | all-gather | bytes 294912 | tf_op jit(solution)/shard_map/all_gather | solution.py:28
  502.0 12.0 %all-reduce.10 = (bf16[1,3,192]{2,0,1:T(2,128)(2,1)S(1)}, bf16[1,192]{1,0:T(2,128)(2,1)S(1)}, bf16[1,768]{1,0:T(2,128)(2,1)S(1)}, bf16[1,192]{1,0:T(2,128)(2,1)S(1)}) all-reduce(bf16[1,3,192]{2,0,1:T(2,128)(2,1)S(1)} %broadcast_in_dim_reshape.22, ...), channel_id=1, replica_groups=mesh['section'=2,'dp'=4,'row'=2,'col'=2] {'dp'}, use_global_device_ids=true, to_apply=%region_105.106 | all-reduce | flops 1728 | bytes 6912 | tf_op jit(solution)/shard_map/psum | solution.py:334
  519.4 31.3 %all-gather.3 = f32[8,2,1152]{2,1,0:T(2,128)S(1)} all-gather(f32[1,2,1152]{2,1,0:T(2,128)S(1)} %fusion.217), channel_id=1, replica_groups=mesh['section'=2,'dp'=4,'row'=2,'col'=2] {'dp','row'}, dimensions={0}, use_global_device_ids=true | all-gather | bytes 82944 | tf_op jit(solution)/shard_map/all_gather | solution.py:343
  550.8 6.1 psum.255
  556.9 26.3 %all-gather.2 = bf16[8,2,384]{2,1,0:T(2,128)(2,1)S(1)} all-gather(bf16[1,2,384]{2,1,0:T(2,128)(2,1)S(1)} %get-tuple-element.201), channel_id=1, replica_groups=mesh['section'=2,'dp'=4,'row'=2,'col'=2] {'dp','row'}, dimensions={0}, use_global_device_ids=true | all-gather | bytes 13824 | tf_op jit(solution)/shard_map/all_gather | solution.py:344
  583.9 30.5 %all-gather.1 = f32[8,2,384]{2,1,0:T(2,128)S(1)} all-gather(f32[1,2,384]{2,1,0:T(2,128)S(1)} %bitcast.377), channel_id=1, replica_groups=mesh['section'=2,'dp'=4,'row'=2,'col'=2] {'dp','row'}, dimensions={0}, use_global_device_ids=true | all-gather | bytes 27648 | tf_op jit(solution)/shard_map/all_gather | solution.py:342
  (635 shorter events, 322.5 us)
Async XLA Ops:
  22.6 29.6 %reduce-scatter.27.cloned.1.call-start = ((), (), s32[]{:S(2)}) async-start(), calls=%async_computation.25 | async-start | bytes 589824 | tf_op jit(solution)/shard_map/reduce_scatter | solution.py:36
  37.6 34.6 %reduce-scatter.29.cloned.1.call-start = ((), (), s32[]{:S(2)}) async-start(), calls=%async_computation.26 | async-start | bytes 2359296 | tf_op jit(solution)/shard_map/reduce_scatter | solution.py:40
  63.0 28.9 %reduce-scatter.31.cloned.1.call-start = ((), (), s32[]{:S(2)}) async-start(), calls=%async_computation.27 | async-start | bytes 589824 | tf_op jit(solution)/shard_map/reduce_scatter | solution.py:36
  77.3 41.7 %reduce-scatter.33.cloned.1.call-start = ((), (), s32[]{:S(2)}) async-start(), calls=%async_computation.28 | async-start | bytes 1769472 | tf_op jit(solution)/shard_map/reduce_scatter | solution.py:40
  109.4 30.4 %reduce-scatter.35.cloned.1.call-start = ((), (), s32[]{:S(2)}) async-start(), calls=%async_computation.29 | async-start | bytes 589824 | tf_op jit(solution)/shard_map/reduce_scatter | solution.py:36
  125.3 27.2 %reduce-scatter.49.cloned.1.call-start = ((), (), s32[]{:S(2)}) async-start(), calls=%async_computation.36 | async-start | bytes 2359296 | tf_op jit(solution)/shard_map/reduce_scatter | solution.py:40
  132.9 31.4 %reduce-scatter.37.cloned.1.call-start = ((), (), s32[]{:S(2)}) async-start(), calls=%async_computation.30 | async-start | bytes 2359296 | tf_op jit(solution)/shard_map/reduce_scatter | solution.py:40
  152.4 33.1 %reduce-scatter.39.cloned.1.call-start = ((), (), s32[]{:S(2)}) async-start(), calls=%async_computation.31 | async-start | bytes 589824 | tf_op jit(solution)/shard_map/reduce_scatter | solution.py:36
  170.8 30.5 %reduce-scatter.51.cloned.1.call-start = ((), (), s32[]{:S(2)}) async-start(), calls=%async_computation.37 | async-start | bytes 589824 | tf_op jit(solution)/shard_map/reduce_scatter | solution.py:36
  174.6 54.3 %reduce-scatter.53.cloned.1.call-start = ((), (), s32[]{:S(2)}) async-start(), calls=%async_computation.38 | async-start | bytes 589824 | tf_op jit(solution)/shard_map/reduce_scatter | solution.py:40
  217.3 26.9 %reduce-scatter.41.cloned.1.call-start = ((), (), s32[]{:S(2)}) async-start(), calls=%async_computation.32 | async-start | bytes 1769472 | tf_op jit(solution)/shard_map/reduce_scatter | solution.py:40
  226.7 30.6 %reduce-scatter.55.cloned.1.call-start = ((), (), s32[]{:S(2)}) async-start(), calls=%async_computation.39 | async-start | bytes 589824 | tf_op jit(solution)/shard_map/reduce_scatter | solution.py:36
  243.9 29.3 %reduce-scatter.43.cloned.1.call-start = ((), (), s32[]{:S(2)}) async-start(), calls=%async_computation.33 | async-start | bytes 589824 | tf_op jit(solution)/shard_map/reduce_scatter | solution.py:36
  251.2 56.3 %reduce-scatter.45.cloned.1.call-start = ((), (), s32[]{:S(2)}) async-start(), calls=%async_computation.34 | async-start | bytes 2359296 | tf_op jit(solution)/shard_map/reduce_scatter | solution.py:40
  288.4 27.3 %reduce-scatter.57.cloned.1.call-start = ((), (), s32[]{:S(2)}) async-start(), calls=%async_computation.40 | async-start | bytes 2359296 | tf_op jit(solution)/shard_map/reduce_scatter | solution.py:40
  307.4 29.4 %reduce-scatter.59.cloned.1.call-start = ((), (), s32[]{:S(2)}) async-start(), calls=%async_computation.41 | async-start | bytes 589824 | tf_op jit(solution)/shard_map/reduce_scatter | solution.py:36
  322.2 39.6 %reduce-scatter.61.cloned.1.call-start = ((), (), s32[]{:S(2)}) async-start(), calls=%async_computation.42 | async-start | bytes 589824 | tf_op jit(solution)/shard_map/reduce_scatter | solution.py:40
  353.8 51.0 %reduce-scatter.63.cloned.1.call-start = ((), (), s32[]{:S(2)}) async-start(), calls=%async_computation.43 | async-start | bytes 589824 | tf_op jit(solution)/shard_map/reduce_scatter | solution.py:36
  377.9 63.9 %reduce-scatter.65.cloned.1.call-start = ((), (), s32[]{:S(2)}) async-start(), calls=%async_computation.44 | async-start | bytes 2359296 | tf_op jit(solution)/shard_map/reduce_scatter | solution.py:40
  428.2 33.8 %reduce-scatter.67.cloned.1.call-start = ((), (), s32[]{:S(2)}) async-start(), calls=%async_computation.45 | async-start | bytes 589824 | tf_op jit(solution)/shard_map/reduce_scatter | solution.py:36
  452.8 26.8 %reduce-scatter.47.cloned.1.call-start = ((), (), s32[]{:S(2)}) async-start(), calls=%async_computation.35 | async-start | bytes 589824 | tf_op jit(solution)/shard_map/reduce_scatter | solution.py:36
  461.4 28.8 %reduce-scatter.69.cloned.1.call-start = ((), (), s32[]{:S(2)}) async-start(), calls=%async_computation.46 | async-start | bytes 589824 | tf_op jit(solution)/shard_map/reduce_scatter | solution.py:40
  477.3 40.4 %reduce-scatter.71.cloned.1.call-start = ((), (), s32[]{:S(2)}) async-start(), calls=%async_computation.47 | async-start | bytes 589824 | tf_op jit(solution)/shard_map/reduce_scatter | solution.py:36
  499.8 124.2 %all-reduce.14.cloned.1.call-start = ((), (), s32[]{:S(2)}) async-start(), calls=%async_computation.48 | async-start | bytes 1966080 | tf_op jit(solution)/shard_map/psum | solution.py:334
  (172 other events, 1889.3 us)
Sparse Core Ops, SparseCore 0:
  22.7 9.9 reduce-scatter.24
  37.7 14.4 reduce-scatter.26
  63.1 9.0 reduce-scatter.28
  77.4 14.4 reduce-scatter.30
  109.5 9.4 reduce-scatter.32
  125.4 14.4 reduce-scatter.34
  142.7 8.9 reduce-scatter.48
  154.0 10.3 reduce-scatter.36
  170.9 14.4 reduce-scatter.38
  188.1 13.1 reduce-scatter.50
  217.4 7.8 reduce-scatter.52
  227.9 9.6 reduce-scatter.40
  244.0 13.2 reduce-scatter.54
  259.9 13.1 reduce-scatter.42
  288.6 9.0 reduce-scatter.44
  307.5 8.1 reduce-scatter.56
  322.3 14.4 reduce-scatter.58
  353.9 7.7 reduce-scatter.60
  378.0 14.3 reduce-scatter.62
  452.9 9.0 reduce-scatter.66
  464.8 14.6 reduce-scatter.46
  482.4 7.8 reduce-scatter.68
  499.9 14.2 reduce-scatter.70
  518.0 50.4 all-reduce.13
  (1 shorter events, 4.9 us)
where the time goes:
time: 639 us; the launch traced here: 636 us
  blocking collectives  251 us (39%)
  waiting for transfers between devices  164 us (26%)
  other arithmetic  85.7 us (13%)
  matrix products  84.8 us (13%)
  local copies, waits for them, and re-layouts  23 us (4%)
  between operations  15.9 us (2%)
  starting transfers between devices  11.1 us (2%)
    reduce_scatter x12, waiting for transfers between devices, rows_total(): return lax.psum_scatter(value, 'row', scatter_dimension=0, tiled=True)  92.3 us
    all_gather x12, blocking collectives, rows_gather(): return lax.all_gather(value, 'row', axis=0, tiled=True)  69.4 us
    reduce_scatter x12, waiting for transfers between devices, cols_total(): return lax.psum_scatter(value, 'col', scatter_dimension=0, tiled=True)  58.9 us
    all_gather x1, blocking collectives, on_device(): dmod_piece = lax.all_gather(dmod_flat, ('dp', 'row'), axis=0, tiled=True)  31.3 us
    all_gather x1, blocking collectives, on_device(): grad_piece = lax.all_gather(cond_grad, ('dp', 'row'), axis=0, tiled=True)  30.5 us
    all_gather x12, blocking collectives, cols_gather(): return lax.all_gather(value, 'col', axis=0, tiled=True)  27.9 us
    psum x10, blocking collectives, feature_sums(): return lax.psum((first, second), 'col')  27 us
    all_gather x1, blocking collectives, on_device(): lax.all_gather(silu_low.astype(jnp.float32), ('dp', 'row'), axis=0, tiled...  26.3 us
  transfers between devices with their start and end apart: 29, of which 20 were waited for; matrix products, arithmetic and copies ran while one was open for 15% of the time, Pallas kernels for 0%

commit v1 on v0

v1 whole, which is shorter than its diff:
```python
import functools
import math

import jax
import jax.numpy as jnp
from jax import lax
from jax.experimental import pallas as pl
from jax.experimental.pallas import tpu as pltpu
from jax.sharding import PartitionSpec as P

D = 384
HALF = D // 2
HEADS = 6
HD = 64
FF = 1536
FFH = FF // 2
SEQ = 256
EPS = 1e-06
SCALE = 1.0 / math.sqrt(HD)
ROWS = 1152
GROWS = 1168
F32 = jnp.float32
BF16 = jnp.bfloat16


def dot(a, b):
    return jnp.dot(a, b, preferred_element_type=F32)


def dot_nt(a, b):
    return lax.dot_general(a, b, (((1,), (1,)), ((), ())), preferred_element_type=F32)


def dot_tn(a, b):
    return lax.dot_general(a, b, (((0,), (0,)), ((), ())), preferred_element_type=F32)


def shard_pieces(r, c):
    out = []
    for p, (pr, pc) in enumerate(((0, 0), (0, HALF), (HALF, 0))):
        out.append(("qkv", (c * HALF, HALF), (p * D + r * HALF, HALF), (pr, HALF), (pc, HALF)))
    out.append(("proj", (r * HALF, HALF), (c * HALF, HALF), (HALF, HALF), (HALF, HALF)))
    for k in range(2):
        out.append(("up", (c * HALF, HALF), (r * FFH + k * D, D), (D + k * HALF, HALF), (0, D)))
        out.append(("down", (r * FFH + k * D, D), (c * HALF, HALF), (2 * D, D), (k * HALF, HALF)))
    return out


def span(pair):
    return slice(pair[0], pair[0] + pair[1])


def norm_rows(v):
    mean_val = jnp.mean(v, axis=-1, keepdims=True)
    cen = v - mean_val
    inv = lax.rsqrt(jnp.mean(cen * cen, axis=-1, keepdims=True) + EPS)
    return cen * inv, inv


def norm_back(g, normed, inv):
    return inv * (
        g
        - jnp.mean(g, axis=-1, keepdims=True)
        - normed * jnp.mean(g * normed, axis=-1, keepdims=True)
    )


C0 = math.sqrt(2.0 / math.pi)


def gelu_parts(v):
    t = jnp.tanh(C0 * (v + 0.044715 * (v * v * v)))
    return 0.5 * v * (1.0 + t), t


def gelu_slope(v, t):
    return 0.5 * (1.0 + t) + 0.5 * v * (1.0 - t * t) * (C0 * (1.0 + 3.0 * 0.044715 * (v * v)))


def softmax(q, k):
    s = dot_nt(q, k) * SCALE
    e = jnp.exp(s - jnp.max(s, axis=-1, keepdims=True))
    return e * (1.0 / jnp.sum(e, axis=-1, keepdims=True))


def head(arr, part, h):
    at = part * D + h * HD
    return arr[:, at : at + HD]


def forward(x, mod, w, b, keep=None):
    def put(name, value):
        if keep is not None:
            keep[name][...] = value

    m = [mod[i : i + 1, :] for i in range(6)]
    normed1, inv1 = norm_rows(x)
    hidden1 = (normed1 * (1.0 + m[1]) + m[0]).astype(BF16)
    packed = (dot(hidden1, w["qkv"][...]) + b["qkv"]).astype(BF16)
    heads = []
    for h in range(HEADS):
        prob = softmax(head(packed, 0, h), head(packed, 1, h))
        heads.append(dot(prob.astype(BF16), head(packed, 2, h)).astype(BF16))
        if keep is not None:
            keep["prob"][h] = prob
    attended = jnp.concatenate(heads, axis=1)
    branch_a = dot(attended, w["proj"][...]) + b["proj"]
    middle = x + m[2] * branch_a
    normed2, inv2 = norm_rows(middle)
    hidden2 = (normed2 * (1.0 + m[4]) + m[3]).astype(BF16)
    pre = dot(hidden2, w["up"][...]) + b["up"]
    act, _ = gelu_parts(pre)
    act = act.astype(BF16)
    branch_f = dot(act, w["down"][...]) + b["down"]
    put("normed1", normed1)
    put("inv1", inv1)
    put("hidden1", hidden1)
    put("packed", packed)
    put("attended", attended)
    put("branch_a", branch_a)
    put("normed2", normed2)
    put("inv2", inv2)
    put("hidden2", hidden2)
    put("pre", pre)
    put("act", act)
    put("branch_f", branch_f)
    return (middle + m[5] * branch_f).astype(BF16)


SAVES = (
    ("normed1", (SEQ, D), F32),
    ("inv1", (SEQ, 1), F32),
    ("hidden1", (SEQ, D), BF16),
    ("packed", (SEQ, 3 * D), BF16),
    ("prob", (HEADS, SEQ, SEQ), F32),
    ("attended", (SEQ, D), BF16),
    ("branch_a", (SEQ, D), F32),
    ("normed2", (SEQ, D), F32),
    ("inv2", (SEQ, 1), F32),
    ("hidden2", (SEQ, D), BF16),
    ("pre", (SEQ, FF), F32),
    ("act", (SEQ, FF), BF16),
    ("branch_f", (SEQ, D), F32),
)
WEIGHTS = (("qkv", (D, 3 * D)), ("proj", (D, D)), ("up", (D, FF)), ("down", (FF, D)))


def col_sum(v):
    return jnp.sum(v.astype(F32), axis=0, keepdims=True)


def backward(grad_out, mod, w, s, put_w=None, put_b=None, dmod=None):
    full = put_w is not None
    m = [mod[i : i + 1, :] for i in range(6)]
    grad_f = (grad_out * m[5]).astype(BF16)
    pre = s["pre"][...]
    _, t = gelu_parts(pre)
    grad_pre = (dot_nt(grad_f, w["down"][...]) * gelu_slope(pre, t)).astype(BF16)
    if full:
        dmod[5:6, :] = col_sum(grad_out * s["branch_f"][...])
        put_w("down", dot_tn(s["act"][...], grad_f).astype(BF16))
        put_b("down", col_sum(grad_f))
    grad_h2 = dot_nt(grad_pre, w["up"][...])
    normed2 = s["normed2"][...]
    if full:
        put_w("up", dot_tn(s["hidden2"][...], grad_pre).astype(BF16))
        put_b("up", col_sum(grad_pre))
        dmod[4:5, :] = col_sum(grad_h2 * normed2)
        dmod[3:4, :] = col_sum(grad_h2)
    grad_mid = grad_out + norm_back(grad_h2 * (1.0 + m[4]), normed2, s["inv2"][...])
    grad_a = (grad_mid * m[2]).astype(BF16)
    if full:
        dmod[2:3, :] = col_sum(grad_mid * s["branch_a"][...])
        put_w("proj", dot_tn(s["attended"][...], grad_a).astype(BF16))
        put_b("proj", col_sum(grad_a))
    grad_att = dot_nt(grad_a, w["proj"][...]).astype(BF16)
    packed = s["packed"][...]
    parts = [[], [], []]
    for h in range(HEADS):
        q, k, v = (head(packed, i, h) for i in range(3))
        prob = s["prob"][h]
        g = grad_att[:, h * HD : (h + 1) * HD]
        grad_prob = dot_nt(g, v)
        delta = jnp.sum(prob * grad_prob, axis=-1, keepdims=True)
        gs = (prob * (grad_prob - delta) * SCALE).astype(BF16)
        parts[0].append(dot(gs, k).astype(BF16))
        parts[1].append(dot_tn(gs, q).astype(BF16))
        parts[2].append(dot_tn(prob.astype(BF16), g).astype(BF16))
    grad_packed = jnp.concatenate(parts[0] + parts[1] + parts[2], axis=1)
    normed1 = s["normed1"][...]
    grad_h1 = dot_nt(grad_packed, w["qkv"][...])
    if full:
        put_w("qkv", dot_tn(s["hidden1"][...], grad_packed).astype(BF16))
        put_b("qkv", col_sum(grad_packed))
        dmod[1:2, :] = col_sum(grad_h1 * normed1)
        dmod[0:1, :] = col_sum(grad_h1)
    return grad_mid + norm_back(grad_h1 * (1.0 + m[1]), normed1, s["inv1"][...])


def first_kernel(x_ref, mod_ref, bq, bp, bu, bd, shards, out_ref, wq, wp, wu, wd):
    w = dict(qkv=wq, proj=wp, up=wu, down=wd)
    for r in range(2):
        for c in range(2):
            for name, fr, fc, pr, pc in shard_pieces(r, c):
                w[name][span(fr), span(fc)] = shards[2 * r + c, span(pr), span(pc)]
    b = dict(qkv=bq[...], proj=bp[...], up=bu[...], down=bd[...])
    out_ref[...] = forward(x_ref[...].astype(F32), mod_ref, w, b)


def second_kernel(x_ref, g_ref, mod_ref, bq, bp, bu, bd, wq, wp, wu, wd, out_ref, gin_ref, *saves):
    w = dict(qkv=wq, proj=wp, up=wu, down=wd)
    s = {name: ref for (name, _, _), ref in zip(SAVES, saves)}
    b = dict(qkv=bq[...], proj=bp[...], up=bu[...], down=bd[...])
    out_ref[...] = forward(x_ref[...].astype(F32), mod_ref, w, b, s)
    gin_ref[...] = backward(g_ref[...].astype(F32), mod_ref, w, s).astype(BF16)


def third_kernel(g_ref, mod_ref, wq, wp, wu, wd, *rest):
    w = dict(qkv=wq, proj=wp, up=wu, down=wd)
    n = len(SAVES)
    s = {name: ref for (name, _, _), ref in zip(SAVES, rest[:n])}
    gin_ref, packed_ref, dmod_ref = rest[n:]
    packed_ref[:, ROWS:, :] = jnp.zeros((4, GROWS - ROWS, D), BF16)

    def put_w(name, value):
        for r in range(2):
            for c in range(2):
                for piece, fr, fc, pr, pc in shard_pieces(r, c):
                    if piece == name:
                        packed_ref[2 * r + c, span(pr), span(pc)] = value[span(fr), span(fc)]

    biases = {}
    put_b = biases.__setitem__
    gin_ref[...] = backward(g_ref[...].astype(F32), mod_ref, w, s, put_w, put_b, dmod_ref)
    zero = jnp.zeros((1, HALF), F32)
    for r in range(2):
        for c in range(2):
            bq = [biases["qkv"][:, p * D + r * HALF : p * D + (r + 1) * HALF] for p in range(3)]
            rows = [
                jnp.concatenate(bq[:2], axis=1),
                jnp.concatenate([bq[2], biases["proj"][:, c * HALF : (c + 1) * HALF]], axis=1),
                biases["up"][:, r * FFH : r * FFH + D],
                biases["up"][:, r * FFH + D : (r + 1) * FFH],
                jnp.concatenate([biases["down"][:, c * HALF : (c + 1) * HALF], zero], axis=1),
                jnp.zeros((GROWS - ROWS - 5, D), F32),
            ]
            packed_ref[2 * r + c, ROWS:, :] = jnp.concatenate(rows, axis=0).astype(BF16)


def call(body, outs, args, flops=2_000_000_000):
    vmem = pl.BlockSpec(memory_space=pltpu.VMEM)
    return pl.pallas_call(
        body,
        out_shape=[jax.ShapeDtypeStruct(s, d) for s, d in outs],
        in_specs=[vmem] * len(args),
        out_specs=[vmem] * len(outs),
        compiler_params=pltpu.CompilerParams(vmem_limit_bytes=60 * 1024 * 1024),
        cost_estimate=pl.CostEstimate(flops=flops, bytes_accessed=8_000_000, transcendentals=800_000),
    )(*args)


def pack(qkv, proj, up, down):
    qkv = qkv.reshape(HALF, 3 * HALF)
    return jnp.concatenate(
        [
            qkv[:, :D],
            jnp.concatenate([qkv[:, D:], proj], axis=1),
            up[:, :D],
            up[:, D:],
            jnp.concatenate([down[:D], down[D:]], axis=1),
        ],
        axis=0,
    )


def on_device(
    latents_in,
    labels,
    timesteps,
    out_grad,
    label_table,
    time_table,
    ada_w,
    ada_b,
    qkv_w,
    qkv_b,
    proj_w,
    proj_b,
    fc1_w,
    fc1_b,
    fc2_w,
    fc2_b,
):
    section_zero = lax.axis_index("section") == 0
    col = lax.axis_index("col")
    swap = [(0, 1), (1, 0)]

    def exchange(a):
        n = a.shape[0] // 2
        mine = lax.dynamic_slice_in_dim(a, col * n, n, 0)
        theirs = lax.ppermute(lax.dynamic_slice_in_dim(a, (1 - col) * n, n, 0), "col", swap)
        first = jnp.where(col == 0, mine, theirs)
        second = jnp.where(col == 0, theirs, mine)
        return jnp.concatenate([first, second], axis=-1)

    def unexchange(a):
        half = a.shape[-1] // 2
        mine = lax.dynamic_slice_in_dim(a, col * half, half, 1)
        theirs = lax.ppermute(lax.dynamic_slice_in_dim(a, (1 - col) * half, half, 1), "col", swap)
        first = jnp.where(col == 0, mine, theirs)
        second = jnp.where(col == 0, theirs, mine)
        return jnp.concatenate([first, second], axis=0)

    shards = lax.all_gather(pack(qkv_w[0], proj_w[0], fc1_w[0], fc2_w[0]), ("row", "col"), axis=0)
    own = latents_in.shape[0] // SEQ
    cond = jnp.concatenate(
        [
            lax.dynamic_slice_in_dim(label_table, labels[i], 1, 0).astype(F32)
            + lax.dynamic_slice_in_dim(time_table, timesteps[i], 1, 0).astype(F32)
            for i in range(own)
        ],
        axis=0,
    )
    silu_low = jax.nn.silu(cond).astype(BF16)
    ada_flat = ada_w[0].reshape(D, 6 * HALF)
    modul_half = dot(silu_low, ada_flat) + ada_b[0].reshape(6 * HALF)
    small = jnp.concatenate(
        [
            modul_half.reshape(own * 6 * HALF),
            qkv_b[0].reshape(3 * HALF),
            proj_b[0],
            fc1_b[0],
            fc2_b[0],
        ]
    )
    everyone = lax.all_gather(small, ("row", "col"), axis=0).reshape(2, 2, -1)
    row = lax.axis_index("row")
    own_row = lax.dynamic_index_in_dim(everyone, row, 0, keepdims=False)
    mods = own_row[:, : own * 6 * HALF].reshape(2, own, 6, HALF)
    mods = lax.dynamic_index_in_dim(mods, col, 1, keepdims=False)
    mod = jnp.concatenate([mods[0], mods[1]], axis=-1)
    at = own * 6 * HALF
    b_qkv = jnp.transpose(everyone[:, 0, at : at + 3 * HALF].reshape(2, 3, HALF), (1, 0, 2)).reshape(1, 3 * D)
    at += 3 * HALF
    b_proj = everyone[0, :, at : at + HALF].reshape(1, D)
    at += HALF
    b_up = everyone[:, 0, at : at + FFH].reshape(1, FF)
    at += FFH
    b_down = everyone[0, :, at : at + HALF].reshape(1, D)
    b = (b_qkv, b_proj, b_up, b_down)

    x = exchange(latents_in)
    cot = exchange(out_grad)
    out1, *w = call(
        first_kernel,
        [((SEQ, D), BF16)] + [(s, BF16) for _, s in WEIGHTS],
        (x, mod, *b, shards),
    )
    received = lax.ppermute(out1, "section", [(0, 1)])
    x2 = jnp.where(section_zero, x, received)
    out, gin1, *saves = call(
        second_kernel,
        [((SEQ, D), BF16), ((SEQ, D), BF16)] + [(s, d) for _, s, d in SAVES],
        (x2, cot, mod, *b, *w),
    )
    grad_back = lax.ppermute(gin1, "section", [(1, 0)])
    cot2 = jnp.where(section_zero, grad_back, cot)
    gin, packed, dmod = call(
        third_kernel,
        [((SEQ, D), F32), ((4, GROWS, D), BF16), ((6, D), F32)],
        (cot2, mod, *w, *saves),
    )
    reduced = lax.psum_scatter(packed, ("row", "col"), scatter_dimension=0, tiled=True)
    reduced = lax.psum(reduced, "dp")[0].astype(F32)

    block_outs = unexchange(out)
    input_grads = unexchange(gin)
    dmod_flat = unexchange(dmod).reshape(own, 6 * HALF)
    dmod_low = dmod_flat.astype(BF16)
    cond_pull = lax.psum(dot_nt(dmod_low, ada_flat), ("section", "col"))
    cond_grad = jax.vjp(jax.nn.silu, cond)[1](cond_pull)[0]
    ids = jnp.stack([labels, timesteps], axis=1)
    ids_all = lax.all_gather(ids, ("dp", "row"), axis=0, tiled=True)
    piece = lax.all_gather(
        jnp.concatenate([cond_grad, dmod_flat, silu_low.astype(F32)], axis=1), ("dp", "row"), axis=0, tiled=True
    )
    grad_piece = piece[:, :D]
    dmod_piece = piece[:, D : D + 6 * HALF]
    silu_piece = piece[:, D + 6 * HALF :].astype(BF16)
    ada_sum = dot_tn(silu_piece, dmod_piece.astype(BF16))
    adab_sum = jnp.sum(dmod_piece, axis=0)

    def table_sum(ids, count):
        hot = (ids[:, None] == jnp.arange(count, dtype=jnp.int32)[None, :]).astype(F32)
        return jnp.einsum("nc,na->ca", hot, grad_piece, precision=lax.Precision.HIGHEST)

    g_qkv = jnp.concatenate([reduced[:HALF], reduced[HALF:D, :HALF]], axis=1)
    g_proj = reduced[HALF:D, HALF:]
    g_up = jnp.concatenate([reduced[D : D + HALF], reduced[D + HALF : 2 * D]], axis=1)
    g_down = jnp.concatenate([reduced[2 * D : 3 * D, :HALF], reduced[2 * D : 3 * D, HALF:]], axis=0)
    tail = reduced[ROWS:]
    return (
        block_outs[None],
        input_grads[None],
        cond_grad,
        table_sum(ids_all[:, 0], label_table.shape[0]),
        table_sum(ids_all[:, 1], time_table.shape[0]),
        ada_sum.reshape(D, 6, HALF)[None],
        adab_sum.reshape(6, HALF)[None],
        g_qkv.reshape(HALF, 3, HALF)[None],
        jnp.concatenate([tail[0], tail[1, :HALF]]).reshape(3, HALF)[None],
        g_proj[None],
        tail[1, HALF:][None],
        g_up[None],
        jnp.concatenate([tail[2], tail[3]])[None],
        g_down[None],
        tail[4, :HALF][None],
    )


def solution(mesh):
    return jax.shard_map(
        on_device,
        mesh=mesh,
        in_specs=(
            P(("dp", "row"), "col"),
            P(("dp", "row")),
            P(("dp", "row")),
            P(("dp", "row"), "col"),
            P(),
            P(),
            P("section", None, None, "col"),
            P("section", None, "col"),
            P("section", "col", None, "row"),
            P("section", None, "row"),
            P("section", "row", "col"),
            P("section", "col"),
            P("section", "col", "row"),
            P("section", "row"),
            P("section", "row", "col"),
            P("section", "col"),
        ),
        out_specs=(
            P("section", ("dp", "row"), "col"),
            P("section", ("dp", "row"), "col"),
            P(("dp", "row"), None),
            P(),
            P(),
            P("section", None, None, "col"),
            P("section", None, "col"),
            P("section", "col", None, "row"),
            P("section", None, "row"),
            P("section", "row", "col"),
            P("section", "col"),
            P("section", "col", "row"),
            P("section", "row"),
            P("section", "row", "col"),
            P("section", "col"),
        ),
        check_vma=False,
    )
```

time: 639 us -> 224 us (0.35)
  blocking collectives: 251 us -> 72.2 us
  waiting for transfers between devices: 164 us -> 52.3 us
  matrix products: 84.8 us -> 6.6 us
  other arithmetic: 85.7 us -> 7.66 us
  Pallas kernels: 0 us -> 31 us
  between operations: 15.9 us -> 22.8 us
    all_gather x28 -> x2, blocking collectives: 206 us -> 50.3 us  [the longest x1 30.6 us: on_device(): lax.all_gather(jnp.concatenate([cond_grad, dmod_flat, silu_low.astype(F32...]
    reduce_scatter x24 -> x1, waiting for transfers between devices: 151 us -> 0.01 us  [on_device(): lax.psum_scatter(packed, ('row', 'col'), scatter_dimension=0, tiled=True)]
    dot_general x64 -> x5, matrix products: 84.8 us -> 6.6 us  [the longest x2 4.41 us: table_sum(): jnp.einsum('nc,na->ca', hot, grad_piece, precision=lax.Precision.HIGHEST)]
    psum x1, waiting for transfers between devices: 0.01 us -> 39 us  [on_device(): reduced = lax.psum(reduced, 'dp')[0].astype(F32)]
    psum x12 -> x1, blocking collectives: 45.1 us -> 6.23 us  [on_device(): cond_pull = lax.psum(dot_nt(dmod_low, ada_flat), ('section', 'col'))]
    pallas_call x0 -> x3, Pallas kernels: none -> 31 us  [call(): pl.pallas_call(body, out_shape=[jax.ShapeDtypeStruct(s, d) for s, d in ou...]
    reduce_sum x29 -> x0, other arithmetic: 27.3 us -> none  [the longest x8 15.3 us: latent_sum(): return jnp.sum(values.reshape(-1, SEQ, values.shape[-1]), axis=1)]
    convert_element_type x28 -> x3, other arithmetic: 26.2 us -> 1.44 us  [the longest x1 1.4 us: on_device(): reduced = lax.psum(reduced, 'dp')[0].astype(F32)]
  transfers between devices with their start and end apart: 29 -> 10, of which waited for: 20 -> 6; matrix products, arithmetic and copies ran while one was open for 15% -> 11% of each run, Pallas kernels for 0% -> 3%
where the time goes in v1:
time: 224 us; the launch traced here: 223 us
  blocking collectives  72.2 us (32%)
  waiting for transfers between devices  52.3 us (23%)
  Pallas kernels  31 us (14%)
  local copies, waits for them, and re-layouts  23.9 us (11%)
  between operations  22.8 us (10%)
  other arithmetic  7.66 us (3%)
  matrix products  6.6 us (3%)
  starting transfers between devices  6.48 us (3%)
    psum x1, waiting for transfers between devices, on_device(): reduced = lax.psum(reduced, 'dp')[0].astype(F32)  39 us
    pallas_call x3, Pallas kernels, call(): pl.pallas_call(body, out_shape=[jax.ShapeDtypeStruct(s, d) for s, d in ou...  31 us
    all_gather x1, blocking collectives, on_device(): lax.all_gather(jnp.concatenate([cond_grad, dmod_flat, silu_low.astype(F32...  30.6 us
    all_gather x1, blocking collectives, on_device(): ids_all = lax.all_gather(ids, ('dp', 'row'), axis=0, tiled=True)  19.7 us
    unnamed x1, blocking collectives  15.7 us
    unnamed x51, local copies, waits for them, and re-layouts  8 us
    ppermute x1, waiting for transfers between devices, on_device(): grad_back = lax.ppermute(gin1, 'section', [(1, 0)])  6.78 us
    psum x1, blocking collectives, on_device(): cond_pull = lax.psum(dot_nt(dmod_low, ada_flat), ('section', 'col'))  6.23 us
  transfers between devices with their start and end apart: 10, of which 6 were waited for; matrix products, arithmetic and copies ran while one was open for 11% of the time, Pallas kernels for 3%

profile of v1, /device:TPU:0, one launch (start us, length us, event | category | flops | bytes accessed | tf_op | source)
XLA Modules:
  0.0 223.0 jit_solution(14199143837000226951)
XLA Ops:
  7.3 1.2 copy.84
  8.5 1.1 copy.86
  10.0 1.2 concatenate.57
  24.5 15.7 %all-reduce = f32[16128]{0:T(1024)S(1)} all-reduce(f32[16128]{0:T(1024)S(1)} %dynamic-update-slice), channel_id=2, replica_groups=mesh['section'=2,'dp'=4,'row'=2,'col'=2] {'row','col'}, use_global_device_ids=true, to_apply=%add | all-reduce | flops 16128 | bytes 129024
  44.8 1.1 all-gather.6.cloned.1.call-done
  45.9 5.8 %copy.87 = bf16[4608,384]{1,0:T(8,128)(2,1)} copy(bf16[4608,384]{0,1:T(8,128)(2,1)} %all-gather.6.cloned.1.call-done) | data formatting | bytes 7077888 | tf_op jit(solution)/shard_map/all_gather | solution.py:314
  51.7 7.4 %shard_map.271 = (bf16[256,384]{1,0:T(8,128)(2,1)}, bf16[384,1152]{1,0:T(8,128)(2,1)}, bf16[384,384]{1,0:T(8,128)(2,1)}, bf16[384,1536]{1,0:T(8,128)(2,1)}, bf16[1536,384]{1,0:T(8,128)(2,1)}) custom-call(bf16[256,384]{1,0:T(8,128)(2,1)} %pad_maximum_fusion.2.x_ref, f32[6,384]{1,0:T(8,128)} %pad_maximum_fusion.6.mod_ref, f32[1,1152]{1,0:T(1,128)} %reshape.72.bq, ...), custom_call_target="tpu_custom_call" | custom-call | flops 2000000000 | bytes 8000000 | tf_op jit(solution)/shard_map/pallas_call | solution.py:252
  59.0 3.6 %collective-permute-start.1 = (bf16[256,384]{1,0:T(8,128)(2,1)}, bf16[256,384]{1,0:T(8,128)(2,1)S(1)}, u32[]{:S(2)}, u32[]{:S(2)}) collective-permute-start(bf16[256,384]{1,0:T(8,128)(2,1)} %get-tuple-element.38), channel_id=1, source_target_pairs={{0,16},{1,17},{2,18},{3,19},{4,20},{5,21},{6,22},{7,23},{8,24},{9,... | collective-permute-start | bytes 589832 | tf_op jit(solution)/shard_map/ppermute | solution.py:359
  63.4 3.8 %collective-permute-done.1 = bf16[256,384]{1,0:T(8,128)(2,1)S(1)} collective-permute-done((bf16[256,384]{1,0:T(8,128)(2,1)}, bf16[256,384]{1,0:T(8,128)(2,1)S(1)}, u32[]{:S(2)}, u32[]{:S(2)}) %collective-permute-start.1) | collective-permute-done | bytes 196640 | tf_op jit(solution)/shard_map/ppermute | solution.py:359
  68.1 11.9 %shard_map.272 = (bf16[256,384]{1,0:T(8,128)(2,1)}, bf16[256,384]{1,0:T(8,128)(2,1)}, f32[256,384]{1,0:T(8,128)}, f32[256,1]{1,0:T(8,128)}, bf16[256,384]{1,0:T(...) custom-call(bf16[256,384]{1,0:T(8,128)(2,1)} %broadcast_select_fusio, ...), custom_call_target="tpu_custom_call" | custom-call | flops 2000000000 | bytes 8000000 | tf_op jit(solution)/shard_map/pallas_call | solution.py:252
  80.0 1.5 collective-permute-start.4
  81.5 6.8 %collective-permute-done.4 = bf16[256,384]{1,0:T(8,128)(2,1)S(1)} collective-permute-done((bf16[256,384]{1,0:T(8,128)(2,1)}, bf16[256,384]{1,0:T(8,128)(2,1)S(1)}, u32[]{:S(2)}, u32[]{:S(2)}) %collective-permute-start.4) | collective-permute-done | bytes 196640 | tf_op jit(solution)/shard_map/ppermute | solution.py:366
  89.1 11.7 %shard_map.273 = (f32[256,384]{1,0:T(8,128)}, bf16[4,1168,384]{2,1,0:T(8,128)(2,1)}, f32[6,384]{1,0:T(8,128)}) custom-call(bf16[256,384]{1,0:T(8,128)(2,1)} %broadcast_select_fusion.g_ref, f32[6,384]{1,0:T(8,128)} %pad_maximum_fusion.6.mod_ref, bf16[384,1152]{1,0:T(8,128)(2,1)} %get-tuple-element.39.wq, bf16[384,384]{1,0:T(8,128)(2,1)} %get-tuple-element.40.wp, ...), custom_call_target="tpu_custom_call" | custom-call | flops 2000000000 | bytes 8000000 | tf_op jit(solution)/shard_map/pallas_call | solution.py:252
  101.0 19.7 %all-gather.2 = s32[8,2,2]{2,1,0:T(2,128)S(1)} all-gather(s32[1,2,2]{2,1,0:T(2,128)S(1)} %bitcast.71), channel_id=1, replica_groups=mesh['section'=2,'dp'=4,'row'=2,'col'=2] {'dp','row'}, dimensions={0}, use_global_device_ids=true | all-gather | bytes 144 | tf_op jit(solution)/shard_map/all_gather | solution.py:383
  121.2 1.1 collective-permute-done.3
  125.0 6.2 %psum.14 = f32[2,384]{1,0:T(2,128)S(1)} all-reduce(f32[2,384]{1,0:T(2,128)S(1)} %fusion.25), channel_id=1, replica_groups=mesh['section'=2,'dp'=4,'row'=2,'col'=2] {'section','col'}, use_global_device_ids=true, to_apply=%region_0.1 | all-reduce | flops 768 | bytes 6144 | tf_op jit(solution)/shard_map/psum | solution.py:380
  131.3 30.6 %all-gather.3 = f32[8,2,1920]{2,1,0:T(2,128)S(1)} all-gather(f32[1,2,1920]{2,1,0:T(2,128)S(1)} %maximum_bitcast_fusion.4), channel_id=1, replica_groups=mesh['section'=2,'dp'=4,'row'=2,'col'=2] {'dp','row'}, dimensions={0}, use_global_device_ids=true | all-gather | bytes 138240 | tf_op jit(solution)/shard_map/all_gather | solution.py:384
  161.9 1.7 fusion.2
  164.3 2.2 fusion
  166.5 2.2 fusion.1
  169.8 39.0 %all-reduce.3.cloned.1.call-done = bf16[1,1168,384]{2,1,0:T(8,128)(2,1)} async-done(((bf16[1,1168,384]{2,1,0:T(8,128)(2,1)}), bf16[1,1168,384]{2,1,0:T(8,128)(2,1)}) %all-reduce.3.cloned.1.call-update) | async-done | bytes 897040 | tf_op jit(solution)/shard_map/psum | solution.py:374
  208.8 1.4 fusion.19
  212.2 1.1 copy.96
  214.6 1.1 copy.97
  (133 shorter events, 21.2 us)
Async XLA Ops:
  7.2 15.0 %copy-start = (bf16[1,384,6,192]{1,3,2,0:T(8,128)(2,1)S(1)}, bf16[1,384,6,192]{1,3,2,0:T(8,128)(2,1)}, u32[]{:S(2)}) copy-start(bf16[1,384,6,192]{1,3,2,0:T(8,128)(2,1)} %param.22) | copy-start | bytes 2654212
  7.2 2.5 %copy-start.6 = (bf16[1,192,192]{2,1,0:T(8,128)(2,1)S(1)}, bf16[1,192,192]{2,1,0:T(8,128)(2,1)}, u32[]{:S(2)}) copy-start(bf16[1,192,192]{2,1,0:T(8,128)(2,1)} %param.26) | copy-start | bytes 221188
  7.2 2.6 %copy-start.3 = (bf16[1,768,192]{1,2,0:T(8,128)(2,1)S(1)}, bf16[1,768,192]{1,2,0:T(8,128)(2,1)}, u32[]{:S(2)}) copy-start(bf16[1,768,192]{1,2,0:T(8,128)(2,1)} %param.30) | copy-start | bytes 884740
  7.2 38.7 %all-gather.6.cloned.1.call-start = ((), (), s32[]{:S(2)}) async-start(), calls=%async_computation.3 | async-start | bytes 4423680 | tf_op jit(solution)/shard_map/all_gather | solution.py:314
  10.0 4.2 %copy-start.11 = (s32[2]{0:T(128)S(1)}, s32[2]{0:T(128)}, u32[]{:S(2)}) copy-start(s32[2]{0:T(128)} %param.18) | copy-start | bytes 28
  10.0 8.7 %copy-start.9 = (f32[1,6,192]{2,0,1:T(1,128)S(1)}, f32[1,6,192]{2,0,1:T(1,128)}, u32[]{:S(2)}) copy-start(f32[1,6,192]{2,0,1:T(1,128)} %param.23) | copy-start | bytes 13828
  11.2 11.4 %copy-start.12 = (f32[1,3,192]{2,0,1:T(1,128)S(1)}, f32[1,3,192]{2,0,1:T(1,128)}, u32[]{:S(2)}) copy-start(f32[1,3,192]{2,0,1:T(1,128)} %param.25) | copy-start | bytes 6916
  11.2 11.5 %copy-start.13 = (f32[1,768]{1,0:T(1,128)S(1)}, f32[1,768]{1,0:T(1,128)}, u32[]{:S(2)}) copy-start(f32[1,768]{1,0:T(1,128)} %param.29) | copy-start | bytes 9220
  11.2 11.5 %copy-start.16 = (u32[32]{0:T(128)S(1)}, u32[32]{0:T(128)}, u32[]{:S(2)}) copy-start(u32[32]{0:T(128)} %constant.54) | copy-start | bytes 388
  11.2 12.8 %copy-start.14 = (f32[1,192]{1,0:T(1,128)S(1)}, f32[1,192]{1,0:T(1,128)}, u32[]{:S(2)}) copy-start(f32[1,192]{1,0:T(1,128)} %param.27) | copy-start | bytes 2308
  11.2 12.8 %copy-start.15 = (f32[1,192]{1,0:T(1,128)S(1)}, f32[1,192]{1,0:T(1,128)}, u32[]{:S(2)}) copy-start(f32[1,192]{1,0:T(1,128)} %param.31) | copy-start | bytes 2308
  11.2 152.3 %reduce-scatter.2.cloned.1.call-start = ((), (), s32[]{:S(2)}) async-start(), calls=%async_computation.1 | async-start | bytes 4485120 | tf_op jit(solution)/shard_map/reduce_scatter | solution.py:373
  11.5 32.5 %collective-permute-start = (bf16[256,192]{1,0:T(8,128)(2,1)S(1)}, bf16[256,192]{1,0:T(8,128)(2,1)S(1)}, u32[]{:S(2)}, u32[]{:S(2)}) collective-permute-start(bf16[256,192]{1,0:T(8,128)(2,1)S(1)} %copy.101), channel_id=1, source_target_pairs={{0,1},{1,0},{2,3},{3,2},{4,5},{5,4},{6,7},{7,6},{8,9},{9,8},{10,11... | collective-permute-start | bytes 294920 | tf_op jit(solution)/shard_map/ppermute | solution.py:301
  12.1 50.5 %collective-permute-start.2 = (bf16[256,192]{1,0:T(8,128)(2,1)S(1)}, bf16[256,192]{1,0:T(8,128)(2,1)S(1)}, u32[]{:S(2)}, u32[]{:S(2)}) collective-permute-start(bf16[256,192]{1,0:T(8,128)(2,1)S(1)} %copy.103), channel_id=1, source_target_pairs={{0,1},{1,0},{2,3},{3,2},{4,5},{5,4},{6,7},{7,6},{8,9},{9,8},{10,11... | collective-permute-start | bytes 294920 | tf_op jit(solution)/shard_map/ppermute | solution.py:301
  59.0 8.2 %collective-permute-start.1 = (bf16[256,384]{1,0:T(8,128)(2,1)}, bf16[256,384]{1,0:T(8,128)(2,1)S(1)}, u32[]{:S(2)}, u32[]{:S(2)}) collective-permute-start(bf16[256,384]{1,0:T(8,128)(2,1)} %get-tuple-element.38), channel_id=1, source_target_pairs={{0,16},{1,17},{2,18},{3,19},{4,20},{5,21},{6,22},{7,23},{8,24},{9,... | collective-permute-start | bytes 589832 | tf_op jit(solution)/shard_map/ppermute | solution.py:359
  80.0 8.3 %collective-permute-start.4 = (bf16[256,384]{1,0:T(8,128)(2,1)}, bf16[256,384]{1,0:T(8,128)(2,1)S(1)}, u32[]{:S(2)}, u32[]{:S(2)}) collective-permute-start(bf16[256,384]{1,0:T(8,128)(2,1)} %get-tuple-element.44), channel_id=1, source_target_pairs={{16,0},{17,1},{18,2},{19,3},{20,4},{21,5},{22,6},{23,7},{24,8},{25... | collective-permute-start | bytes 589832 | tf_op jit(solution)/shard_map/ppermute | solution.py:366
  100.8 20.0 %copy-start.2 = (bf16[256,384]{1,0:T(8,128)(2,1)S(1)}, bf16[256,384]{1,0:T(8,128)(2,1)}, u32[]{:S(2)}) copy-start(bf16[256,384]{1,0:T(8,128)(2,1)} %get-tuple-element.43) | copy-start | bytes 589828
  100.8 22.4 %copy-start.7 = (f32[6,384]{1,0:T(8,128)S(1)}, f32[6,384]{1,0:T(8,128)}, u32[]{:S(2)}) copy-start(f32[6,384]{1,0:T(8,128)} %get-tuple-element.59) | copy-start | bytes 27652
  100.8 22.7 %copy-start.1 = (f32[256,384]{1,0:T(8,128)S(1)}, f32[256,384]{1,0:T(8,128)}, u32[]{:S(2)}) copy-start(f32[256,384]{1,0:T(8,128)} %get-tuple-element.58) | copy-start | bytes 1179652
  100.8 108.0 %all-reduce.3.cloned.1.call-start = ((), (), s32[]{:S(2)}) async-start(), calls=%async_computation.2 | async-start | bytes 1794048 | tf_op jit(solution)/shard_map/psum | solution.py:374
  120.9 1.4 collective-permute-start.3
  123.3 1.2 collective-permute-start.6
  123.6 45.1 %collective-permute-start.5 = (f32[256,192]{1,0:T(8,128)S(1)}, f32[256,192]{1,0:T(8,128)S(1)}, u32[]{:S(2)}, u32[]{:S(2)}) collective-permute-start(f32[256,192]{1,0:T(8,128)S(1)} %constant_dynamic-slice_fusion.1), channel_id=1, source_target_pairs={{0,1},{1,0},{2,3},{3,2},{4,5},{5,4},{6,7},{7,6},{8,9},{9,8},{10,11... | collective-permute-start | bytes 589832 | tf_op jit(solution)/shard_map/ppermute | solution.py:309
  131.2 35.3 %copy-start.8 = (f32[2,384]{1,0:T(2,128)}, f32[2,384]{1,0:T(2,128)S(1)}, u32[]{:S(2)}) copy-start(f32[2,384]{1,0:T(2,128)S(1)} %get-tuple-element.163) | copy-start | bytes 9220
  (3 other events, 5.1 us)
Sparse Core Ops, SparseCore 0:
  11.4 34.4 all-gather.5
  100.9 40.3 reduce-scatter.1
  163.7 45.0 all-reduce.2

commit v2 on v1

--- a/solution.py
+++ b/solution.py
@@ -18,7 +18,9 @@
 EPS = 1e-06
 SCALE = 1.0 / math.sqrt(HD)
 ROWS = 1152
-GROWS = 1168
+GROWS = 1184
+CHUNKS = ((0, 320), (320, 320), (640, 288), (928, 256))
+MESH = pl.DeviceIdType.MESH
 F32 = jnp.float32
 BF16 = jnp.bfloat16
 
@@ -157,7 +159,7 @@
     _, t = gelu_parts(pre)
     grad_pre = (dot_nt(grad_f, w["down"][...]) * gelu_slope(pre, t)).astype(BF16)
     if full:
-        dmod[5:6, :] = col_sum(grad_out * s["branch_f"][...])
+        dmod[5] = col_sum(grad_out * s["branch_f"][...])
         put_w("down", dot_tn(s["act"][...], grad_f).astype(BF16))
         put_b("down", col_sum(grad_f))
     grad_h2 = dot_nt(grad_pre, w["up"][...])
@@ -165,12 +167,12 @@
     if full:
         put_w("up", dot_tn(s["hidden2"][...], grad_pre).astype(BF16))
         put_b("up", col_sum(grad_pre))
-        dmod[4:5, :] = col_sum(grad_h2 * normed2)
-        dmod[3:4, :] = col_sum(grad_h2)
+        dmod[4] = col_sum(grad_h2 * normed2)
+        dmod[3] = col_sum(grad_h2)
     grad_mid = grad_out + norm_back(grad_h2 * (1.0 + m[4]), normed2, s["inv2"][...])
     grad_a = (grad_mid * m[2]).astype(BF16)
     if full:
-        dmod[2:3, :] = col_sum(grad_mid * s["branch_a"][...])
+        dmod[2] = col_sum(grad_mid * s["branch_a"][...])
         put_w("proj", dot_tn(s["attended"][...], grad_a).astype(BF16))
         put_b("proj", col_sum(grad_a))
     grad_att = dot_nt(grad_a, w["proj"][...]).astype(BF16)
@@ -192,8 +194,8 @@
     if full:
         put_w("qkv", dot_tn(s["hidden1"][...], grad_packed).astype(BF16))
         put_b("qkv", col_sum(grad_packed))
-        dmod[1:2, :] = col_sum(grad_h1 * normed1)
-        dmod[0:1, :] = col_sum(grad_h1)
+        dmod[1] = col_sum(grad_h1 * normed1)
+        dmod[0] = col_sum(grad_h1)
     return grad_mid + norm_back(grad_h1 * (1.0 + m[1]), normed1, s["inv1"][...])
 
 
@@ -211,7 +213,9 @@
     w = dict(qkv=wq, proj=wp, up=wu, down=wd)
     s = {name: ref for (name, _, _), ref in zip(SAVES, saves)}
     b = dict(qkv=bq[...], proj=bp[...], up=bu[...], down=bd[...])
-    out_ref[...] = forward(x_ref[...].astype(F32), mod_ref, w, b, s)
+    out = forward(x_ref[...].astype(F32), mod_ref, w, b, s)
+    for c in range(2):
+        out_ref[c] = out[:, c * HALF : (c + 1) * HALF]
     gin_ref[...] = backward(g_ref[...].astype(F32), mod_ref, w, s).astype(BF16)
 
 
@@ -231,7 +235,13 @@
 
     biases = {}
     put_b = biases.__setitem__
-    gin_ref[...] = backward(g_ref[...].astype(F32), mod_ref, w, s, put_w, put_b, dmod_ref)
+    dmod_ref[...] = jnp.zeros_like(dmod_ref)
+    dmod = {}
+    gin = backward(g_ref[...].astype(F32), mod_ref, w, s, put_w, put_b, dmod)
+    for c in range(2):
+        gin_ref[c] = gin[:, c * HALF : (c + 1) * HALF]
+        for i in range(6):
+            dmod_ref[c, i : i + 1, :] = dmod[i][:, c * HALF : (c + 1) * HALF]
     zero = jnp.zeros((1, HALF), F32)
     for r in range(2):
         for c in range(2):
@@ -256,6 +266,271 @@
         out_specs=[vmem] * len(outs),
         compiler_params=pltpu.CompilerParams(vmem_limit_bytes=60 * 1024 * 1024),
         cost_estimate=pl.CostEstimate(flops=flops, bytes_accessed=8_000_000, transcendentals=800_000),
+    )(*args)
+
+
+def flipped(index, step):
+    return index + step * (1 - 2 * lax.rem(index // step, 2))
+
+
+def greet(partners):
+    barrier = pltpu.get_barrier_semaphore()
+    for where in partners:
+        pl.semaphore_signal(barrier, inc=1, device_id=where, device_id_type=MESH)
+    pl.semaphore_wait(barrier, len(partners))
+
+
+class Wires:
+    def __init__(self, send_sem, recv_sem):
+        self.send_sem, self.recv_sem, self.started = send_sem, recv_sem, []
+
+    def send(self, k, src, dst, where):
+        copy = pltpu.make_async_remote_copy(
+            src_ref=src,
+            dst_ref=dst,
+            send_sem=self.send_sem.at[k],
+            recv_sem=self.recv_sem.at[k],
+            device_id=where,
+            device_id_type=MESH,
+        )
+        copy.start()
+        self.started.append(copy)
+
+    def arrived(self, k, dst, where):
+        pltpu.make_async_remote_copy(
+            src_ref=dst,
+            dst_ref=dst,
+            send_sem=self.send_sem.at[k],
+            recv_sem=self.recv_sem.at[k],
+            device_id=where,
+            device_id_type=MESH,
+        ).wait_recv()
+
+    def finish(self):
+        for copy in self.started:
+            copy.wait_send()
+
+
+PIECE = 192
+PIECES = ROWS // 2 // PIECE
+
+
+def gather_kernel(
+    shard, lat, cot, labels, times, ltab, ttab, ada, adab, bias,
+    out, x_out, cot_out, mod_out, bias_out, silu_out, cond_out,
+    xr, cr, modbuf, biasbuf, send_sem, recv_sem,
+):
+    r, c, z = lax.axis_index("row"), lax.axis_index("col"), lax.axis_index("dp")
+    h = lax.rem(z, 2)
+    to_col, to_row, to_dp = {"col": 1 - c}, {"row": 1 - r}, {"dp": flipped(z, 1)}
+    greet((to_col, to_row, to_dp))
+    wires = Wires(send_sem, recv_sem)
+    own, facing = 2 * r + c, 2 * (1 - r) + c
+
+    def rows(half, i):
+        return pl.ds(pl.multiple_of(half * (ROWS // 2) + i * PIECE, PIECE), PIECE)
+
+    for i in range(PIECES):
+        wires.send(i, shard.at[rows(h, i)], out.at[own, rows(h, i)], to_row)
+    theirs = pl.ds(pl.multiple_of((1 - c) * SEQ, SEQ), SEQ)
+    mine = pl.ds(pl.multiple_of(c * SEQ, SEQ), SEQ)
+    base = 2 * PIECES
+    wires.send(base, lat.at[theirs], xr.at[c], to_col)
+    wires.send(base + 1, cot.at[theirs], cr.at[c], to_col)
+    wires.send(base + 2, shard, out.at[own], to_col)
+    wires.send(base + 3, bias, biasbuf.at[0], to_col)
+    wires.send(base + 4, bias, biasbuf.at[1], to_row)
+    out[own] = shard[...]
+    xr[c] = lat[mine, :]
+    cr[c] = cot[mine, :]
+
+    def hot(ids, table):
+        grid = lax.broadcasted_iota(jnp.int32, (ids.shape[0], table.shape[0]), 1)
+        return dot(jnp.where(grid == ids[...], 1.0, 0.0).astype(BF16), table[...])
+
+    cond = hot(labels, ltab) + hot(times, ttab)
+    cond_out[...] = cond
+    silu_low = (cond / (1.0 + jnp.exp(-cond))).astype(BF16)
+    silu_out[...] = silu_low.astype(F32)
+    modul = dot(silu_low, ada[...]) + adab[...]
+    modbuf[0:2] = jnp.zeros((2, 8, HALF), F32)
+    for latent in range(2):
+        for i in range(6):
+            modbuf[latent, i : i + 1, :] = modul[latent : latent + 1, i * HALF : (i + 1) * HALF]
+    far = base + 6
+    for i in range(PIECES):
+        wires.arrived(i, out.at[facing, rows(h, i)], to_row)
+        wires.send(PIECES + i, out.at[facing, rows(h, i)], out.at[facing, rows(h, i)], to_dp)
+        wires.send(far + i, out.at[facing, rows(h, i)], out.at[facing, rows(h, i)], to_col)
+        if i == 0:
+            wires.send(base + 5, modbuf.at[1 - c], modbuf.at[2 + c], to_col)
+    for i in range(PIECES):
+        wires.arrived(PIECES + i, out.at[facing, rows(1 - h, i)], to_dp)
+        wires.send(far + PIECES + i, out.at[facing, rows(1 - h, i)], out.at[facing, rows(1 - h, i)], to_col)
+    wires.arrived(base, xr.at[1 - c], to_col)
+    wires.arrived(base + 1, cr.at[1 - c], to_col)
+    wires.arrived(base + 3, biasbuf.at[0], to_col)
+    wires.arrived(base + 4, biasbuf.at[1], to_row)
+    wires.arrived(base + 5, modbuf.at[2 + 1 - c], to_col)
+    modbuf[2 + c] = modbuf[c]
+    bias_out[...] = biasbuf[...]
+    for half in range(2):
+        x_out[:, half * HALF : (half + 1) * HALF] = xr[half]
+        cot_out[:, half * HALF : (half + 1) * HALF] = cr[half]
+        mod_out[:, half * HALF : (half + 1) * HALF] = modbuf[2 + half]
+    wires.arrived(base + 2, out.at[2 * r + 1 - c], to_col)
+    for i in range(PIECES):
+        wires.arrived(far + i, out.at[2 * (1 - r) + 1 - c, rows(h, i)], to_col)
+    for i in range(PIECES):
+        wires.arrived(far + PIECES + i, out.at[2 * (1 - r) + 1 - c, rows(1 - h, i)], to_col)
+    wires.finish()
+
+
+def reduce_kernel(
+    bits, packed, outs, gin, dmod, cond, silu, labels, times, ada,
+    g_qkv, g_proj, g_up, g_down, tail, block_out, input_grad, table, cond_grad,
+    rc, t1, own1, rr, t2, acc, rz, res, dm, pull, send_sem, recv_sem,
+):
+    r, c, z = lax.axis_index("row"), lax.axis_index("col"), lax.axis_index("dp")
+    b = lax.rem(z, 2)
+    sec = lax.axis_index("section")
+    to_col, to_row, to_sec = {"col": 1 - c}, {"row": 1 - r}, {"section": 1 - sec}
+    to_dp = [{"dp": flipped(z, 1 << j)} for j in range(bits)]
+    greet((to_col, to_row, to_sec, *to_dp))
+    wires = Wires(send_sem, recv_sem)
+    count = len(CHUNKS)
+    number = iter(range(1000))
+    n_col = [[next(number) for _ in range(2)] for _ in CHUNKS]
+    n_row = [next(number) for _ in CHUNKS]
+    n_dp = [[next(number) for _ in range(bits)] for _ in CHUNKS]
+    n_back = [next(number) for _ in CHUNKS]
+    n_dm, n_p0, n_p1, n_out, n_gin = (next(number) for _ in range(5))
+    n_table = [next(number) for _ in range(bits + 1)]
+
+    def rows(k):
+        return pl.ds(CHUNKS[k][0], CHUNKS[k][1])
+
+    def half(k, which):
+        size = CHUNKS[k][1] // 2
+        return pl.ds(pl.multiple_of(CHUNKS[k][0] + which * size, 16), size)
+
+    wires.send(n_dm, dmod.at[1 - c], dm.at[c], to_col)
+    for k in range(count):
+        for which, q in enumerate((1 - r, r)):
+            wires.send(n_col[k][which], packed.at[2 * q + 1 - c, rows(k)], rc.at[q, rows(k)], to_col)
+    mine = pl.ds(pl.multiple_of(c * SEQ, SEQ), SEQ)
+    others = pl.ds(pl.multiple_of((1 - c) * SEQ, SEQ), SEQ)
+    wires.send(n_out, outs.at[1 - c], block_out.at[mine], to_col)
+    wires.send(n_gin, gin.at[1 - c], input_grad.at[mine], to_col)
+
+    def total(left, right):
+        return (left.astype(F32) + right.astype(F32)).astype(BF16)
+
+    def from_col(k):
+        wires.arrived(n_col[k][0], rc.at[1 - r, rows(k)], to_col)
+        t1[rows(k), :] = total(packed[2 * (1 - r) + c, rows(k), :], rc[1 - r, rows(k), :])
+        wires.send(n_row[k], t1.at[rows(k)], rr.at[rows(k)], to_row)
+        wires.arrived(n_col[k][1], rc.at[r, rows(k)], to_col)
+        own1[rows(k), :] = total(packed[2 * r + c, rows(k), :], rc[r, rows(k), :])
+
+    def from_row(k):
+        wires.arrived(n_row[k], rr.at[rows(k)], to_row)
+        t2[rows(k), :] = total(own1[rows(k), :], rr[rows(k), :])
+        wires.send(n_dp[k][0], t2.at[half(k, 1 - b)], rz.at[0, half(k, 1 - b)], to_dp[0])
+
+    def from_dp(k, j):
+        keep = half(k, b)
+        wires.arrived(n_dp[k][j], rz.at[j, keep], to_dp[j])
+        prior = t2[keep, :] if j == 0 else acc[j - 1, keep, :]
+        value = total(prior, rz[j, keep, :])
+        if j < bits - 1:
+            acc[j, keep, :] = value
+            wires.send(n_dp[k][j + 1], acc.at[j, keep], rz.at[j + 1, keep], to_dp[j + 1])
+        else:
+            res[keep, :] = value
+            wires.send(n_back[k], res.at[keep], res.at[keep], to_dp[0])
+
+    def pull_part():
+        wires.arrived(n_dm, dm.at[1 - c], to_col)
+        dm[c] = dmod[c]
+        pull[0] = jnp.zeros((8, D), F32)
+        for latent in range(2):
+            low = dm[latent].astype(BF16)
+            part = jnp.zeros((8, D), F32)
+            for i in range(6):
+                part += dot_nt(jnp.broadcast_to(low[i : i + 1, :], (8, HALF)), ada[:, i * HALF : (i + 1) * HALF])
+            pull[0, latent : latent + 1, :] = part[:1]
+
+    def pull_col():
+        wires.send(n_p0, pull.at[0], pull.at[1], to_col)
+
+    def pull_section():
+        wires.arrived(n_p0, pull.at[1], to_col)
+        pull[2] = pull[0] + pull[1]
+        wires.send(n_p1, pull.at[2], pull.at[3], to_sec)
+
+    me = 2 * z + r
+
+    def fill_table():
+        wires.arrived(n_p1, pull.at[3], to_sec)
+        v = cond[...]
+        sig = 1.0 / (1.0 + jnp.exp(-v))
+        grad = (pull[2, 0:2, :] + pull[3, 0:2, :]) * (sig * (1.0 + v * (1.0 - sig)))
+        cond_grad[...] = grad
+        ids = [jnp.broadcast_to(ref[...].astype(F32), (2, D)) for ref in (labels, times)]
+        mods = jnp.concatenate([dm[0, 0:6, :], dm[1, 0:6, :]], axis=1)
+        table[me] = jnp.concatenate([grad, mods, silu[...], *ids, jnp.zeros((2, D), F32)], axis=0)
+
+    def share_table(j):
+        size = 1 << j
+        block = pl.ds((me // size) * size, size)
+        if j > 0:
+            low = size // 2
+            other = pl.ds(flipped(me // low, 1) * low, low)
+            wires.arrived(n_table[j - 1], table.at[other], to_row if j == 1 else to_dp[j - 2])
+        if j <= bits:
+            wires.send(n_table[j], table.at[block], table.at[block], to_row if j == 0 else to_dp[j - 1])
+
+    extra = [pull_part, pull_col, pull_section, fill_table]
+    extra += [functools.partial(share_table, j) for j in range(bits + 2)]
+    stages = [from_col, from_row] + [lambda k, j=j: from_dp(k, j) for j in range(bits)]
+    for tick in range(max(count + len(stages), len(extra))):
+        for stage, step in enumerate(stages):
+            if 0 <= tick - stage < count:
+                step(tick - stage)
+        if tick < len(extra):
+            extra[tick]()
+    block_out[mine, :] = outs[c]
+    input_grad[mine, :] = gin[c]
+    wires.arrived(n_out, block_out.at[others], to_col)
+    wires.arrived(n_gin, input_grad.at[others], to_col)
+    for k in range(count):
+        wires.arrived(n_back[k], res.at[half(k, 1 - b)], to_dp[0])
+    g_qkv[:, :D] = res[:HALF, :].astype(F32)
+    low = res[HALF:D, :].astype(F32)
+    g_qkv[:, D:] = low[:, :HALF]
+    g_proj[...] = low[:, HALF:]
+    g_up[:, :D] = res[D : D + HALF, :].astype(F32)
+    g_up[:, D:] = res[D + HALF : 2 * D, :].astype(F32)
+    low = res[2 * D : 3 * D, :].astype(F32)
+    g_down[:D, :] = low[:, :HALF]
+    g_down[D:, :] = low[:, HALF:]
+    tail[...] = res[ROWS:, :].astype(F32)
+    wires.finish()
+
+
+def remote_call(body, outs, scratch, args, wires, collective_id):
+    vmem = pl.BlockSpec(memory_space=pltpu.VMEM)
+    return pl.pallas_call(
+        body,
+        out_shape=[jax.ShapeDtypeStruct(s, d) for s, d in outs],
+        in_specs=[vmem] * len(args),
+        out_specs=[vmem] * len(outs),
+        scratch_shapes=[pltpu.VMEM(s, d) for s, d in scratch]
+        + [pltpu.SemaphoreType.DMA((wires,)), pltpu.SemaphoreType.DMA((wires,))],
+        compiler_params=pltpu.CompilerParams(
+            vmem_limit_bytes=60 * 1024 * 1024, collective_id=collective_id, has_side_effects=True
+        ),
     )(*args)
 
 
@@ -292,65 +567,45 @@
     fc2_b,
 ):
     section_zero = lax.axis_index("section") == 0
-    col = lax.axis_index("col")
-    swap = [(0, 1), (1, 0)]
-
-    def exchange(a):
-        n = a.shape[0] // 2
-        mine = lax.dynamic_slice_in_dim(a, col * n, n, 0)
-        theirs = lax.ppermute(lax.dynamic_slice_in_dim(a, (1 - col) * n, n, 0), "col", swap)
-        first = jnp.where(col == 0, mine, theirs)
-        second = jnp.where(col == 0, theirs, mine)
-        return jnp.concatenate([first, second], axis=-1)
-
-    def unexchange(a):
-        half = a.shape[-1] // 2
-        mine = lax.dynamic_slice_in_dim(a, col * half, half, 1)
-        theirs = lax.ppermute(lax.dynamic_slice_in_dim(a, (1 - col) * half, half, 1), "col", swap)
-        first = jnp.where(col == 0, mine, theirs)
-        second = jnp.where(col == 0, theirs, mine)
-        return jnp.concatenate([first, second], axis=0)
-
-    shards = lax.all_gather(pack(qkv_w[0], proj_w[0], fc1_w[0], fc2_w[0]), ("row", "col"), axis=0)
     own = latents_in.shape[0] // SEQ
-    cond = jnp.concatenate(
+    places = lax.axis_size("dp") * lax.axis_size("row")
+    bits = lax.axis_size("dp").bit_length() - 1
+    shard = pack(qkv_w[0], proj_w[0], fc1_w[0], fc2_w[0])
+    ada_flat = ada_w[0].reshape(D, 6 * HALF)
+    zero = jnp.zeros((HALF,), F32)
+    bias = jnp.concatenate([qkv_b[0].reshape(3 * HALF), proj_b[0], fc1_b[0], fc2_b[0], zero]).reshape(5, D)
+    bias = jnp.concatenate([bias, jnp.zeros((3, D), F32)], axis=0)
+    labels2, times2 = labels[:, None], timesteps[:, None]
+    shards, x, cot, mod, other_bias, silu, cond = remote_call(
+        gather_kernel,
         [
-            lax.dynamic_slice_in_dim(label_table, labels[i], 1, 0).astype(F32)
-            + lax.dynamic_slice_in_dim(time_table, timesteps[i], 1, 0).astype(F32)
-            for i in range(own)
+            ((4, ROWS, D), BF16),
+            ((SEQ, D), BF16),
+            ((SEQ, D), BF16),
+            ((8, D), F32),
+            ((2, 8, D), F32),
+            ((own, D), F32),
+            ((own, D), F32),
         ],
-        axis=0,
-    )
-    silu_low = jax.nn.silu(cond).astype(BF16)
-    ada_flat = ada_w[0].reshape(D, 6 * HALF)
-    modul_half = dot(silu_low, ada_flat) + ada_b[0].reshape(6 * HALF)
-    small = jnp.concatenate(
-        [
-            modul_half.reshape(own * 6 * HALF),
-            qkv_b[0].reshape(3 * HALF),
-            proj_b[0],
-            fc1_b[0],
-            fc2_b[0],
-        ]
-    )
-    everyone = lax.all_gather(small, ("row", "col"), axis=0).reshape(2, 2, -1)
-    row = lax.axis_index("row")
-    own_row = lax.dynamic_index_in_dim(everyone, row, 0, keepdims=False)
-    mods = own_row[:, : own * 6 * HALF].reshape(2, own, 6, HALF)
-    mods = lax.dynamic_index_in_dim(mods, col, 1, keepdims=False)
-    mod = jnp.concatenate([mods[0], mods[1]], axis=-1)
-    at = own * 6 * HALF
-    b_qkv = jnp.transpose(everyone[:, 0, at : at + 3 * HALF].reshape(2, 3, HALF), (1, 0, 2)).reshape(1, 3 * D)
-    at += 3 * HALF
-    b_proj = everyone[0, :, at : at + HALF].reshape(1, D)
-    at += HALF
-    b_up = everyone[:, 0, at : at + FFH].reshape(1, FF)
-    at += FFH
-    b_down = everyone[0, :, at : at + HALF].reshape(1, D)
+        [((2, SEQ, HALF), BF16), ((2, SEQ, HALF), BF16), ((4, 8, HALF), F32), ((2, 8, D), F32)],
+        (shard, latents_in, out_grad, labels2, times2, label_table, time_table, ada_flat, ada_b[0].reshape(1, 6 * HALF), bias),
+        4 * PIECES + 6,
+        0,
+    )
+    flat = bias.reshape(-1)
+    col_flat, row_flat = other_bias[0].reshape(-1), other_bias[1].reshape(-1)
+    row_one, col_one = lax.axis_index("row") == 1, lax.axis_index("col") == 1
+
+    def ordered(is_second, other, at, size):
+        mine, theirs = flat[at : at + size], other[at : at + size]
+        return jnp.where(is_second, theirs, mine), jnp.where(is_second, mine, theirs)
+
+    low, high = ordered(row_one, row_flat, 0, 3 * HALF)
+    b_qkv = jnp.concatenate([low.reshape(3, HALF), high.reshape(3, HALF)], axis=1).reshape(1, 3 * D)
+    b_proj = jnp.concatenate(ordered(col_one, col_flat, 3 * HALF, HALF)).reshape(1, D)
+    b_up = jnp.concatenate(ordered(row_one, row_flat, 4 * HALF, FFH)).reshape(1, FF)
+    b_down = jnp.concatenate(ordered(col_one, col_flat, 4 * HALF + FFH, HALF)).reshape(1, D)
     b = (b_qkv, b_proj, b_up, b_down)
-
-    x = exchange(latents_in)
-    cot = exchange(out_grad)
     out1, *w = call(
         first_kernel,
         [((SEQ, D), BF16)] + [(s, BF16) for _, s in WEIGHTS],
@@ -360,51 +615,64 @@
     x2 = jnp.where(section_zero, x, received)
     out, gin1, *saves = call(
         second_kernel,
-        [((SEQ, D), BF16), ((SEQ, D), BF16)] + [(s, d) for _, s, d in SAVES],
+        [((2, SEQ, HALF), BF16), ((SEQ, D), BF16)] + [(s, d) for _, s, d in SAVES],
         (x2, cot, mod, *b, *w),
     )
     grad_back = lax.ppermute(gin1, "section", [(1, 0)])
     cot2 = jnp.where(section_zero, grad_back, cot)
     gin, packed, dmod = call(
         third_kernel,
-        [((SEQ, D), F32), ((4, GROWS, D), BF16), ((6, D), F32)],
+        [((2, SEQ, HALF), F32), ((4, GROWS, D), BF16), ((2, 8, HALF), F32)],
         (cot2, mod, *w, *saves),
     )
-    reduced = lax.psum_scatter(packed, ("row", "col"), scatter_dimension=0, tiled=True)
-    reduced = lax.psum(reduced, "dp")[0].astype(F32)
-
-    block_outs = unexchange(out)
-    input_grads = unexchange(gin)
-    dmod_flat = unexchange(dmod).reshape(own, 6 * HALF)
-    dmod_low = dmod_flat.astype(BF16)
-    cond_pull = lax.psum(dot_nt(dmod_low, ada_flat), ("section", "col"))
-    cond_grad = jax.vjp(jax.nn.silu, cond)[1](cond_pull)[0]
-    ids = jnp.stack([labels, timesteps], axis=1)
-    ids_all = lax.all_gather(ids, ("dp", "row"), axis=0, tiled=True)
-    piece = lax.all_gather(
-        jnp.concatenate([cond_grad, dmod_flat, silu_low.astype(F32)], axis=1), ("dp", "row"), axis=0, tiled=True
-    )
-    grad_piece = piece[:, :D]
-    dmod_piece = piece[:, D : D + 6 * HALF]
-    silu_piece = piece[:, D + 6 * HALF :].astype(BF16)
+    vmem_half = ((GROWS, D), BF16)
+    g_qkv, g_proj, g_up, g_down, tail, block_outs, input_grads, table, cond_grad = remote_call(
+        functools.partial(reduce_kernel, bits),
+        [
+            ((HALF, 3 * HALF), F32),
+            ((HALF, HALF), F32),
+            ((HALF, FFH), F32),
+            ((FFH, HALF), F32),
+            ((GROWS - ROWS, D), F32),
+            ((own * SEQ, HALF), BF16),
+            ((own * SEQ, HALF), F32),
+            ((places, 16, D), F32),
+            ((own, D), F32),
+        ],
+        [
+            ((2, GROWS, D), BF16),
+            vmem_half,
+            vmem_half,
+            vmem_half,
+            vmem_half,
+            ((bits, GROWS, D), BF16),
+            ((bits, GROWS, D), BF16),
+            vmem_half,
+            ((2, 8, HALF), F32),
+            ((4, 8, D), F32),
+        ],
+        (packed, out, gin, dmod, cond, silu, labels2, times2, ada_flat),
+        len(CHUNKS) * (4 + bits) + 5 + bits + 1,
+        1,
+    )
+    grad_piece = table[:, 0:2].reshape(-1, D)
+    dmod_piece = jnp.transpose(table[:, 2:8].reshape(places, 6, own, HALF), (0, 2, 1, 3)).reshape(-1, 6 * HALF)
+    silu_piece = table[:, 8:10].reshape(-1, D).astype(BF16)
+    label_ids = table[:, 10:12, 0].reshape(-1)
+    step_ids = table[:, 12:14, 0].reshape(-1)
     ada_sum = dot_tn(silu_piece, dmod_piece.astype(BF16))
     adab_sum = jnp.sum(dmod_piece, axis=0)
 
     def table_sum(ids, count):
-        hot = (ids[:, None] == jnp.arange(count, dtype=jnp.int32)[None, :]).astype(F32)
+        hot = (ids[:, None] == jnp.arange(count, dtype=jnp.int32).astype(F32)[None, :]).astype(F32)
         return jnp.einsum("nc,na->ca", hot, grad_piece, precision=lax.Precision.HIGHEST)
 
-    g_qkv = jnp.concatenate([reduced[:HALF], reduced[HALF:D, :HALF]], axis=1)
-    g_proj = reduced[HALF:D, HALF:]
-    g_up = jnp.concatenate([reduced[D : D + HALF], reduced[D + HALF : 2 * D]], axis=1)
-    g_down = jnp.concatenate([reduced[2 * D : 3 * D, :HALF], reduced[2 * D : 3 * D, HALF:]], axis=0)
-    tail = reduced[ROWS:]
     return (
         block_outs[None],
         input_grads[None],
         cond_grad,
-        table_sum(ids_all[:, 0], label_table.shape[0]),
-        table_sum(ids_all[:, 1], time_table.shape[0]),
+        table_sum(label_ids, label_table.shape[0]),
+        table_sum(step_ids, time_table.shape[0]),
         ada_sum.reshape(D, 6, HALF)[None],
         adab_sum.reshape(6, HALF)[None],
         g_qkv.reshape(HALF, 3, HALF)[None],

time: 224 us -> 166 us (0.74)
  Pallas kernels: 31 us -> 110 us
  blocking collectives: 72.2 us -> 0 us
  waiting for transfers between devices: 52.3 us -> 11.7 us
  between operations: 22.8 us -> 1.03 us
  other arithmetic: 7.66 us -> 3.43 us
  local copies, waits for them, and re-layouts: 23.9 us -> 27.4 us
    pallas_call x0 -> x2, Pallas kernels: none -> 79 us  [remote_call(): pl.pallas_call(body, out_shape=[jax.ShapeDtypeStruct(s, d) for s, d in ou...]
    all_gather x2 -> x0, blocking collectives: 50.3 us -> none  [the longest x1 30.6 us: on_device(): lax.all_gather(jnp.concatenate([cond_grad, dmod_flat, silu_low.astype(F32...]
    psum x1 -> x0, waiting for transfers between devices: 39 us -> none  [on_device(): reduced = lax.psum(reduced, 'dp')[0].astype(F32)]
    unnamed x1 -> x0, blocking collectives: 15.7 us -> none
    psum x1 -> x0, blocking collectives: 6.23 us -> none  [on_device(): cond_pull = lax.psum(dot_nt(dmod_low, ada_flat), ('section', 'col'))]
    all_gather x1 -> x0, local copies, waits for them, and re-layouts: 5.76 us -> none  [on_device(): lax.all_gather(pack(qkv_w[0], proj_w[0], fc1_w[0], fc2_w[0]), ('row', 'co...]
    unnamed x51 -> x58, local copies, waits for them, and re-layouts: 8 us -> 11.2 us
    slice x9 -> x10, local copies, waits for them, and re-layouts: 2.17 us -> 5.23 us  [the longest x1 0.92 us: on_device(): step_ids = table[:, 12:14, 0].reshape(-1)]
  transfers between devices with their start and end apart: 10 -> 2, of which waited for: 6 -> 2; matrix products, arithmetic and copies ran while one was open for 11% -> 0% of each run, Pallas kernels for 3% -> 0%
where the time goes in v2:
time: 166 us; the launch traced here: 165 us
  Pallas kernels  110 us (66%)
  local copies, waits for them, and re-layouts  27.4 us (17%)
  waiting for transfers between devices  11.7 us (7%)
  matrix products  6.08 us (4%)
  starting transfers between devices  5.1 us (3%)
  other arithmetic  3.43 us (2%)
    pallas_call x2, Pallas kernels, remote_call(): pl.pallas_call(body, out_shape=[jax.ShapeDtypeStruct(s, d) for s, d in ou...  79 us
    pallas_call x3, Pallas kernels, call(): pl.pallas_call(body, out_shape=[jax.ShapeDtypeStruct(s, d) for s, d in ou...  31.1 us
    unnamed x58, local copies, waits for them, and re-layouts  11.2 us
    ppermute x1, waiting for transfers between devices, on_device(): grad_back = lax.ppermute(gin1, 'section', [(1, 0)])  6.93 us
    ppermute x1, waiting for transfers between devices, on_device(): received = lax.ppermute(out1, 'section', [(0, 1)])  4.81 us
    dot_general x2, matrix products, table_sum(): jnp.einsum('nc,na->ca', hot, grad_piece, precision=lax.Precision.HIGHEST)  4.43 us
    ppermute x1, starting transfers between devices, on_device(): received = lax.ppermute(out1, 'section', [(0, 1)])  3.59 us
  transfers between devices with their start and end apart: 2, of which 2 were waited for; matrix products, arithmetic and copies ran while one was open for 0% of the time, Pallas kernels for 0%

profile of v2, /device:TPU:0, one launch (start us, length us, event | category | flops | bytes accessed | tf_op | source)
XLA Modules:
  0.0 164.9 jit_solution(14628972296338663077)
XLA Ops:
  0.7 1.2 copy.45
  5.4 1.5 copy.54.ada
  10.7 0.9 copy-done
  11.6 24.6 %shard_map.271 = (bf16[4,1152,384]{2,1,0:T(8,128)(2,1)}, bf16[256,384]{1,0:T(8,128)(2,1)}, bf16[256,384]{1,0:T(8,128)(2,1)}, f32[8,384]{1,0:T(8,128)}, f32[2,8,3...) custom-call(bf16[1152,384]{1,0:T(8,128)(2,1)} %copy-done, bf16[512,192]{1,0:T(8,128)(2,1)} %copy.50.lat, ...), custom_call_target="tpu_custom_call" | custom-call | tf_op jit(solution)/shard_map/pallas_call | solution.py:524
  40.3 7.4 %shard_map.272 = (bf16[256,384]{1,0:T(8,128)(2,1)}, bf16[384,1152]{1,0:T(8,128)(2,1)}, bf16[384,384]{1,0:T(8,128)(2,1)}, bf16[384,1536]{1,0:T(8,128)(2,1)}, bf16[1536,384]{1,0:T(8,128)(2,1)}) custom-call(bf16[256,384]{1,0:T(8,128)(2,1)} %get-tuple-element.54.x_ref, f32[8,384]{1,0:T(8,128)} %get-tuple-element.55.mod_ref, f32[1,1152]{1,0:T(1,128)} %bitcast.49, ...), custom_call_target="tpu_custom_call" | custom-call | flops 2000000000 | bytes 8000000 | tf_op jit(solution)/shard_map/pallas_call | solution.py:262
  47.7 3.6 %collective-permute-start = (bf16[256,384]{1,0:T(8,128)(2,1)}, bf16[256,384]{1,0:T(8,128)(2,1)S(1)}, u32[]{:S(2)}, u32[]{:S(2)}) collective-permute-start(bf16[256,384]{1,0:T(8,128)(2,1)} %get-tuple-element.58), channel_id=1, source_target_pairs={{0,16},{1,17},{2,18},{3,19},{4,20},{5,21},{6,22},{7,23},{8,24},{9,... | collective-permute-start | bytes 589832 | tf_op jit(solution)/shard_map/ppermute | solution.py:614
  51.3 4.8 %collective-permute-done = bf16[256,384]{1,0:T(8,128)(2,1)S(1)} collective-permute-done((bf16[256,384]{1,0:T(8,128)(2,1)}, bf16[256,384]{1,0:T(8,128)(2,1)S(1)}, u32[]{:S(2)}, u32[]{:S(2)}) %collective-permute-start) | collective-permute-done | bytes 196640 | tf_op jit(solution)/shard_map/ppermute | solution.py:614
  56.9 11.8 %shard_map.273 = (bf16[2,256,192]{2,1,0:T(8,128)(2,1)}, bf16[256,384]{1,0:T(8,128)(2,1)}, f32[256,384]{1,0:T(8,128)}, f32[256,1]{1,0:T(8,128)}, bf16[256,384]{1,...) custom-call(bf16[256,384]{1,0:T(8,128)(2,1)} %broadcast_select_fusio, ...), custom_call_target="tpu_custom_call" | custom-call | flops 2000000000 | bytes 8000000 | tf_op jit(solution)/shard_map/pallas_call | solution.py:262
  68.7 1.5 collective-permute-start.1
  70.2 6.9 %collective-permute-done.1 = bf16[256,384]{1,0:T(8,128)(2,1)S(1)} collective-permute-done((bf16[256,384]{1,0:T(8,128)(2,1)}, bf16[256,384]{1,0:T(8,128)(2,1)S(1)}, u32[]{:S(2)}, u32[]{:S(2)}) %collective-permute-start.1) | collective-permute-done | bytes 196640 | tf_op jit(solution)/shard_map/ppermute | solution.py:621
  77.8 11.9 %shard_map.274 = (f32[2,256,192]{2,1,0:T(8,128)}, bf16[4,1184,384]{2,1,0:T(8,128)(2,1)}, f32[2,8,192]{2,1,0:T(8,128)}) custom-call(bf16[256,384]{1,0:T(8,128)(2,1)} %broadcast_select_fusion.g_ref, f32[8,384]{1,0:T(8,128)} %get-tuple-element.55.mod_ref, bf16[384,1152]{1,0:T(8,128)(2,1)} %get-tuple-element.60.wq, bf16[384,384]{1,0:T(8,128)(2,1)} %get-tuple-element.61.wp, ...), custom_call_target="tpu_custom_call" | custom-call | flops 2000000000 | bytes 8000000 | tf_op jit(solution)/shard_map/pallas_call | solution.py:262
  89.7 54.4 %shard_map.275 = (f32[192,576]{1,0:T(8,128)}, f32[192,192]{1,0:T(8,128)}, f32[192,768]{1,0:T(8,128)}, f32[768,192]{1,0:T(8,128)}, f32[32,384]{1,0:T(8,128)}, /*i...) custom-call(bf16[4,1184,384]{2,1,0:T(8,128)(2,1)} %get-tuple-element.78.packed, ...), custom_call_target="tpu_custom_call" | custom-call | tf_op jit(solution)/shard_map/pallas_call | solution.py:524
  144.1 0.8 slice_reduce_fusion.3
  145.0 1.4 fusion.10
  146.4 0.9 slice.125
  147.3 0.9 slice.163
  148.2 0.9 slice.122
  149.1 0.9 slice_reduce_fusion
  152.0 2.2 %fusion = f32[1000,384]{1,0:T(8,128)} fusion(f32[16,384]{1,0:T(8,128)S(1)} %reshape.93, f32[1000]{0:T(1024)S(1)} %iota_convert_fusion, f32[16]{0:T(128)S(1)} %eq.46), kind=kOutput, calls=%fused_computation.9 | convolution fusion | flops 73744000 | bytes 1564640 | tf_op jit(solution)/shard_map/nc,na->ca/dot_general | solution.py:668
  154.2 2.2 %fusion.2 = f32[1000,384]{1,0:T(8,128)} fusion(f32[16,384]{1,0:T(8,128)S(1)} %reshape.93, f32[1000]{0:T(1024)S(1)} %iota_convert_fusion, f32[16]{0:T(128)S(1)} %eq.42), kind=kOutput, calls=%fused_computation.11 | convolution fusion | flops 73744000 | bytes 1564640 | tf_op jit(solution)/shard_map/nc,na->ca/dot_general | solution.py:668
  156.7 1.1 copy.64
  157.8 1.1 copy.65
  158.8 0.9 copy.63
  161.2 1.7 %convolution_bitcast_fusion = f32[1,384,6,192]{1,3,2,0:T(8,128)} fusion(bf16[16,384,1]{1,0,2:T(8,128)(2,1)S(1)} %reshape.95, bf16[6,192,16]{1,0,2:T(8,128)(2,1)S(1)} %dot_general.18), kind=kOutput, calls=%fused_computation | convolution fusion | flops 14155776 | bytes 1818624 | tf_op jit(solution)/shard_map/dot_general | solution.py:37
  (105 shorter events, 18.3 us)
Async XLA Ops:
  0.6 3.9 %copy-start.15 = (bf16[1,192,192]{2,1,0:T(8,128)(2,1)S(1)}, bf16[1,192,192]{2,1,0:T(8,128)(2,1)}, u32[]{:S(2)}) copy-start(bf16[1,192,192]{2,1,0:T(8,128)(2,1)} %param.26) | copy-start | bytes 221188
  0.7 4.0 %copy-start.6 = (bf16[1,192,768]{2,1,0:T(8,128)(2,1)S(1)}, bf16[1,192,768]{2,1,0:T(8,128)(2,1)}, u32[]{:S(2)}) copy-start(bf16[1,192,768]{2,1,0:T(8,128)(2,1)} %param.28) | copy-start | bytes 884740
  0.7 4.1 %copy-start.7 = (bf16[1,768,192]{1,2,0:T(8,128)(2,1)S(1)}, bf16[1,768,192]{1,2,0:T(8,128)(2,1)}, u32[]{:S(2)}) copy-start(bf16[1,768,192]{1,2,0:T(8,128)(2,1)} %param.30) | copy-start | bytes 884740
  4.2 1.2 copy-start.1
  4.2 2.7 %copy-start.14 = (f32[8,384]{1,0:T(8,128)}, f32[8,384]{1,0:T(8,128)S(1)}, u32[]{:S(2)}) copy-start(f32[8,384]{1,0:T(8,128)S(1)} %concatenate.37.bias) | copy-start | bytes 36868
  4.8 2.1 %copy-start.18 = (s32[2]{0:T(128)S(1)}, s32[2]{0:T(128)}, u32[]{:S(2)}) copy-start(s32[2]{0:T(128)} %param.17) | copy-start | bytes 28
  4.8 2.7 %copy-start.19 = (s32[2]{0:T(128)S(1)}, s32[2]{0:T(128)}, u32[]{:S(2)}) copy-start(s32[2]{0:T(128)} %param.18) | copy-start | bytes 28
  4.8 3.4 %copy-start.9 = (bf16[512,192]{0,1:T(8,128)(2,1)S(1)}, bf16[512,192]{0,1:T(8,128)(2,1)}, u32[]{:S(2)}) copy-start(bf16[512,192]{0,1:T(8,128)(2,1)} %param.16) | copy-start | bytes 589828
  4.9 4.2 %copy-start.10 = (bf16[512,192]{0,1:T(8,128)(2,1)S(1)}, bf16[512,192]{0,1:T(8,128)(2,1)}, u32[]{:S(2)}) copy-start(bf16[512,192]{0,1:T(8,128)(2,1)} %param.19) | copy-start | bytes 589828
  5.0 4.9 %copy-start.16 = (f32[1,6,192]{2,0,1:T(1,128)S(1)}, f32[1,6,192]{2,0,1:T(1,128)}, u32[]{:S(2)}) copy-start(f32[1,6,192]{2,0,1:T(1,128)} %param.23) | copy-start | bytes 13828
  10.7 0.9 copy-start
  40.3 15.8 %copy-start.13 = (bf16[256,384]{1,0:T(8,128)(2,1)S(1)}, bf16[256,384]{1,0:T(8,128)(2,1)}, u32[]{:S(2)}) copy-start(bf16[256,384]{1,0:T(8,128)(2,1)} %get-tuple-element.54.x_ref) | copy-start | bytes 589828
  47.7 8.4 %collective-permute-start = (bf16[256,384]{1,0:T(8,128)(2,1)}, bf16[256,384]{1,0:T(8,128)(2,1)S(1)}, u32[]{:S(2)}, u32[]{:S(2)}) collective-permute-start(bf16[256,384]{1,0:T(8,128)(2,1)} %get-tuple-element.58), channel_id=1, source_target_pairs={{0,16},{1,17},{2,18},{3,19},{4,20},{5,21},{6,22},{7,23},{8,24},{9,... | collective-permute-start | bytes 589832 | tf_op jit(solution)/shard_map/ppermute | solution.py:614
  56.9 20.3 %copy-start.12 = (bf16[256,384]{1,0:T(8,128)(2,1)S(1)}, bf16[256,384]{1,0:T(8,128)(2,1)}, u32[]{:S(2)}) copy-start(bf16[256,384]{1,0:T(8,128)(2,1)} %get-tuple-element.59.g_ref) | copy-start | bytes 589828
  68.7 8.5 %collective-permute-start.1 = (bf16[256,384]{1,0:T(8,128)(2,1)}, bf16[256,384]{1,0:T(8,128)(2,1)S(1)}, u32[]{:S(2)}, u32[]{:S(2)}) collective-permute-start(bf16[256,384]{1,0:T(8,128)(2,1)} %get-tuple-element.64), channel_id=1, source_target_pairs={{16,0},{17,1},{18,2},{19,3},{20,4},{21,5},{22,6},{23,7},{24,8},{25... | collective-permute-start | bytes 589832 | tf_op jit(solution)/shard_map/ppermute | solution.py:621
  151.9 4.6 %copy-start.5 = (f32[192,576]{1,0:T(8,128)S(1)}, f32[192,576]{1,0:T(8,128)}, u32[]{:S(2)}) copy-start(f32[192,576]{1,0:T(8,128)} %get-tuple-element.88) | copy-start | bytes 1327108
  154.2 3.5 %copy-start.2 = (f32[768,192]{1,0:T(8,128)S(1)}, f32[768,192]{1,0:T(8,128)}, u32[]{:S(2)}) copy-start(f32[768,192]{1,0:T(8,128)} %get-tuple-element.92) | copy-start | bytes 1769476
  156.5 2.4 %copy-start.4 = (f32[512,192]{1,0:T(8,128)S(1)}, f32[512,192]{1,0:T(8,128)}, u32[]{:S(2)}) copy-start(f32[512,192]{1,0:T(8,128)} %get-tuple-element.85) | copy-start | bytes 1179652
  156.7 3.7 %copy-start.8 = (bf16[512,192]{1,0:T(8,128)(2,1)S(1)}, bf16[512,192]{1,0:T(8,128)(2,1)}, u32[]{:S(2)}) copy-start(bf16[512,192]{1,0:T(8,128)(2,1)} %get-tuple-element.84) | copy-start | bytes 589828
  158.8 4.0 %copy-start.17 = (f32[2,384]{1,0:T(2,128)S(1)}, f32[2,384]{1,0:T(2,128)}, u32[]{:S(2)}) copy-start(f32[2,384]{1,0:T(2,128)} %get-tuple-element.162) | copy-start | bytes 9220
  158.8 4.6 %copy-start.11 = (f32[192,192]{1,0:T(8,128)S(1)}, f32[192,192]{1,0:T(8,128)}, u32[]{:S(2)}) copy-start(f32[192,192]{1,0:T(8,128)} %get-tuple-element.90) | copy-start | bytes 442372
  159.8 4.3 %copy-start.3 = (f32[192,768]{1,0:T(8,128)S(1)}, f32[192,768]{1,0:T(8,128)}, u32[]{:S(2)}) copy-start(f32[192,768]{1,0:T(8,128)} %get-tuple-element.91) | copy-start | bytes 1769476

commit v3 on v2

--- a/solution.py
+++ b/solution.py
@@ -534,6 +534,33 @@
     )(*args)
 
 
+def final_kernel(table, label_out, time_out, ada_out, adab_out):
+    def hot_sum(at, count):
+        total = jnp.zeros((count, D), F32)
+        for l in range(2):
+            ids = table[:, at + l, :][:, 0:1]
+            grid = lax.broadcasted_iota(jnp.int32, (ids.shape[0], count), 1).astype(F32)
+            total += lax.dot_general(
+                jnp.where(grid == ids, 1.0, 0.0),
+                table[:, l, :],
+                (((0,), (0,)), ((), ())),
+                preferred_element_type=F32,
+                precision=lax.Precision.HIGHEST,
+            )
+        return total
+
+    label_out[...] = hot_sum(10, label_out.shape[0])
+    time_out[...] = hot_sum(12, time_out.shape[0])
+    for i in range(6):
+        mods = table[:, 2 + i, :]
+        total = jnp.zeros((D, HALF), F32)
+        for l in range(2):
+            total += dot_tn(table[:, 8 + l, :].astype(BF16), mods[:, l * HALF : (l + 1) * HALF].astype(BF16))
+        ada_out[:, i, :] = total
+        sums = jnp.sum(mods, axis=0, keepdims=True)
+        adab_out[i : i + 1, :] = sums[:, :HALF] + sums[:, HALF:]
+
+
 def pack(qkv, proj, up, down):
     qkv = qkv.reshape(HALF, 3 * HALF)
     return jnp.concatenate(
@@ -655,26 +682,19 @@
         len(CHUNKS) * (4 + bits) + 5 + bits + 1,
         1,
     )
-    grad_piece = table[:, 0:2].reshape(-1, D)
-    dmod_piece = jnp.transpose(table[:, 2:8].reshape(places, 6, own, HALF), (0, 2, 1, 3)).reshape(-1, 6 * HALF)
-    silu_piece = table[:, 8:10].reshape(-1, D).astype(BF16)
-    label_ids = table[:, 10:12, 0].reshape(-1)
-    step_ids = table[:, 12:14, 0].reshape(-1)
-    ada_sum = dot_tn(silu_piece, dmod_piece.astype(BF16))
-    adab_sum = jnp.sum(dmod_piece, axis=0)
-
-    def table_sum(ids, count):
-        hot = (ids[:, None] == jnp.arange(count, dtype=jnp.int32).astype(F32)[None, :]).astype(F32)
-        return jnp.einsum("nc,na->ca", hot, grad_piece, precision=lax.Precision.HIGHEST)
-
+    label_sum, time_sum, ada_sum, adab_sum = call(
+        final_kernel,
+        [(label_table.shape, F32), (time_table.shape, F32), ((D, 6, HALF), F32), ((6, HALF), F32)],
+        (table,),
+    )
     return (
         block_outs[None],
         input_grads[None],
         cond_grad,
-        table_sum(label_ids, label_table.shape[0]),
-        table_sum(step_ids, time_table.shape[0]),
-        ada_sum.reshape(D, 6, HALF)[None],
-        adab_sum.reshape(6, HALF)[None],
+        label_sum,
+        time_sum,
+        ada_sum[None],
+        adab_sum[None],
         g_qkv.reshape(HALF, 3, HALF)[None],
         jnp.concatenate([tail[0], tail[1, :HALF]]).reshape(3, HALF)[None],
         g_proj[None],

time: 166 us -> 175 us (1.054)
  Pallas kernels: 110 us -> 121 us
  matrix products: 6.08 us -> 0 us
  local copies, waits for them, and re-layouts: 27.4 us -> 31.5 us
    pallas_call x3 -> x4, Pallas kernels: 31.1 us -> 41.6 us  [call(): pl.pallas_call(body, out_shape=[jax.ShapeDtypeStruct(s, d) for s, d in ou...]
    unnamed x58 -> x48, local copies, waits for them, and re-layouts: 11.2 us -> 18.7 us
    dot_general x3 -> x0, matrix products: 6.08 us -> none  [the longest x2 4.43 us: table_sum(): jnp.einsum('nc,na->ca', hot, grad_piece, precision=lax.Precision.HIGHEST)]
    slice x5 -> x0, local copies, waits for them, and re-layouts: 3.64 us -> none  [the longest x1 0.92 us: on_device(): step_ids = table[:, 12:14, 0].reshape(-1)]
where the time goes in v3:
time: 175 us; the launch traced here: 174 us
  Pallas kernels  121 us (69%)
  local copies, waits for them, and re-layouts  31.5 us (18%)
  waiting for transfers between devices  11.8 us (7%)
  starting transfers between devices  5.09 us (3%)
  other arithmetic  4.1 us (2%)
    pallas_call x2, Pallas kernels, remote_call(): pl.pallas_call(body, out_shape=[jax.ShapeDtypeStruct(s, d) for s, d in ou...  79 us
    pallas_call x4, Pallas kernels, call(): pl.pallas_call(body, out_shape=[jax.ShapeDtypeStruct(s, d) for s, d in ou...  41.6 us
    unnamed x48, local copies, waits for them, and re-layouts  18.7 us
    ppermute x1, waiting for transfers between devices, on_device(): grad_back = lax.ppermute(gin1, 'section', [(1, 0)])  6.94 us
    ppermute x1, waiting for transfers between devices, on_device(): received = lax.ppermute(out1, 'section', [(0, 1)])  4.82 us
    ppermute x1, starting transfers between devices, on_device(): received = lax.ppermute(out1, 'section', [(0, 1)])  3.57 us
  transfers between devices with their start and end apart: 2, of which 2 were waited for; matrix products, arithmetic and copies ran while one was open for 0% of the time, Pallas kernels for 0%

profile of v3, /device:TPU:0, one launch (start us, length us, event | category | flops | bytes accessed | tf_op | source)
XLA Modules:
  0.0 173.9 jit_solution(11528442652667963622)
XLA Ops:
  3.1 1.1 copy.47
  4.3 1.3 copy.54.labels
  5.6 1.3 copy.55.times
  8.3 1.8 %copy.52.lat = bf16[512,192]{1,0:T(8,128)(2,1)} copy(bf16[512,192]{0,1:T(8,128)(2,1)} %param.16) | data formatting | bytes 393216 | tf_op args[0]
  12.1 1.5 copy.56.ada
  13.8 0.9 copy-done
  14.7 24.6 %shard_map.271 = (bf16[4,1152,384]{2,1,0:T(8,128)(2,1)}, bf16[256,384]{1,0:T(8,128)(2,1)}, bf16[256,384]{1,0:T(8,128)(2,1)}, f32[8,384]{1,0:T(8,128)}, f32[2,8,3...) custom-call(bf16[1152,384]{1,0:T(8,128)(2,1)} %copy-done, bf16[512,192]{1,0:T(8,128)(2,1)} %copy.52.lat, ...), custom_call_target="tpu_custom_call" | custom-call | tf_op jit(solution)/shard_map/pallas_call | solution.py:524
  43.4 7.4 %shard_map.272 = (bf16[256,384]{1,0:T(8,128)(2,1)}, bf16[384,1152]{1,0:T(8,128)(2,1)}, bf16[384,384]{1,0:T(8,128)(2,1)}, bf16[384,1536]{1,0:T(8,128)(2,1)}, bf16[1536,384]{1,0:T(8,128)(2,1)}) custom-call(bf16[256,384]{1,0:T(8,128)(2,1)} %get-tuple-element.58.x_ref, f32[8,384]{1,0:T(8,128)} %get-tuple-element.59.mod_ref, f32[1,1152]{1,0:T(1,128)} %bitcast.39, ...), custom_call_target="tpu_custom_call" | custom-call | flops 2000000000 | bytes 8000000 | tf_op jit(solution)/shard_map/pallas_call | solution.py:262
  50.8 3.6 %collective-permute-start = (bf16[256,384]{1,0:T(8,128)(2,1)}, bf16[256,384]{1,0:T(8,128)(2,1)S(1)}, u32[]{:S(2)}, u32[]{:S(2)}) collective-permute-start(bf16[256,384]{1,0:T(8,128)(2,1)} %get-tuple-element.62), channel_id=1, source_target_pairs={{0,16},{1,17},{2,18},{3,19},{4,20},{5,21},{6,22},{7,23},{8,24},{9,... | collective-permute-start | bytes 589832 | tf_op jit(solution)/shard_map/ppermute | solution.py:641
  54.4 4.8 %collective-permute-done = bf16[256,384]{1,0:T(8,128)(2,1)S(1)} collective-permute-done((bf16[256,384]{1,0:T(8,128)(2,1)}, bf16[256,384]{1,0:T(8,128)(2,1)S(1)}, u32[]{:S(2)}, u32[]{:S(2)}) %collective-permute-start) | collective-permute-done | bytes 196640 | tf_op jit(solution)/shard_map/ppermute | solution.py:641
  59.9 11.8 %shard_map.273 = (bf16[2,256,192]{2,1,0:T(8,128)(2,1)}, bf16[256,384]{1,0:T(8,128)(2,1)}, f32[256,384]{1,0:T(8,128)}, f32[256,1]{1,0:T(8,128)}, bf16[256,384]{1,...) custom-call(bf16[256,384]{1,0:T(8,128)(2,1)} %broadcast_select_fusio, ...), custom_call_target="tpu_custom_call" | custom-call | flops 2000000000 | bytes 8000000 | tf_op jit(solution)/shard_map/pallas_call | solution.py:262
  71.7 1.5 collective-permute-start.1
  73.2 6.9 %collective-permute-done.1 = bf16[256,384]{1,0:T(8,128)(2,1)S(1)} collective-permute-done((bf16[256,384]{1,0:T(8,128)(2,1)}, bf16[256,384]{1,0:T(8,128)(2,1)S(1)}, u32[]{:S(2)}, u32[]{:S(2)}) %collective-permute-start.1) | collective-permute-done | bytes 196640 | tf_op jit(solution)/shard_map/ppermute | solution.py:648
  80.9 11.9 %shard_map.274 = (f32[2,256,192]{2,1,0:T(8,128)}, bf16[4,1184,384]{2,1,0:T(8,128)(2,1)}, f32[2,8,192]{2,1,0:T(8,128)}) custom-call(bf16[256,384]{1,0:T(8,128)(2,1)} %broadcast_select_fusion.g_ref, f32[8,384]{1,0:T(8,128)} %get-tuple-element.59.mod_ref, bf16[384,1152]{1,0:T(8,128)(2,1)} %get-tuple-element.64.wq, bf16[384,384]{1,0:T(8,128)(2,1)} %get-tuple-element.65.wp, ...), custom_call_target="tpu_custom_call" | custom-call | flops 2000000000 | bytes 8000000 | tf_op jit(solution)/shard_map/pallas_call | solution.py:262
  92.8 54.4 %shard_map.275 = (f32[192,576]{1,0:T(8,128)}, f32[192,192]{1,0:T(8,128)}, f32[192,768]{1,0:T(8,128)}, f32[768,192]{1,0:T(8,128)}, f32[32,384]{1,0:T(8,128)}, /*i...) custom-call(bf16[4,1184,384]{2,1,0:T(8,128)(2,1)} %get-tuple-element.82.packed, ...), custom_call_target="tpu_custom_call" | custom-call | tf_op jit(solution)/shard_map/pallas_call | solution.py:524
  147.2 1.4 fusion.1
  148.6 0.8 slice_reduce_fusion.1
  149.5 1.8 %copy.61 = bf16[1,512,192]{1,2,0:T(8,128)(2,1)} copy(bf16[1,512,192]{2,1,0:T(8,128)(2,1)} %bitcast.35) | data formatting | bytes 393216
  151.2 2.0 %copy.62 = f32[1,512,192]{1,2,0:T(8,128)} copy(f32[1,512,192]{2,1,0:T(8,128)} %bitcast.32) | data formatting | bytes 786432
  154.7 1.1 copy.65
  155.8 1.1 copy.66
  156.9 10.5 %shard_map.276 = (f32[1000,384]{1,0:T(8,128)}, f32[1000,384]{1,0:T(8,128)}, f32[384,6,192]{2,1,0:T(8,128)}, f32[6,192]{1,0:T(8,128)}) custom-call(f32[8,16,384]{2,1,0:T(8,128)} %get-tuple-element.91.table), custom_call_target="tpu_custom_call" | custom-call | flops 2000000000 | bytes 8000000 | tf_op jit(solution)/shard_map/pallas_call | solution.py:262
  167.4 1.3 copy.64
  168.7 3.1 %copy.63 = f32[1,384,6,192]{1,3,2,0:T(8,128)} copy(f32[1,384,6,192]{3,2,1,0:T(8,128)} %bitcast.23) | data formatting | bytes 3538944
  (76 shorter events, 15.0 us)
Async XLA Ops:
  0.6 9.4 %copy-start.7 = (bf16[512,192]{0,1:T(8,128)(2,1)S(1)}, bf16[512,192]{0,1:T(8,128)(2,1)}, u32[]{:S(2)}) copy-start(bf16[512,192]{0,1:T(8,128)(2,1)} %param.19) | copy-start | bytes 589828
  0.7 10.5 %copy-start.5 = (bf16[1,768,192]{1,2,0:T(8,128)(2,1)S(1)}, bf16[1,768,192]{1,2,0:T(8,128)(2,1)}, u32[]{:S(2)}) copy-start(bf16[1,768,192]{1,2,0:T(8,128)(2,1)} %param.30) | copy-start | bytes 884740
  3.0 8.2 %copy-start.11 = (f32[8,384]{1,0:T(8,128)}, f32[8,384]{1,0:T(8,128)S(1)}, u32[]{:S(2)}) copy-start(f32[8,384]{1,0:T(8,128)S(1)} %concatenate.37.bias) | copy-start | bytes 36868
  4.3 7.3 %copy-start.12 = (bf16[1,192,192]{2,1,0:T(8,128)(2,1)S(1)}, bf16[1,192,192]{2,1,0:T(8,128)(2,1)}, u32[]{:S(2)}) copy-start(bf16[1,192,192]{2,1,0:T(8,128)(2,1)} %param.26) | copy-start | bytes 221188
  10.1 1.6 copy-start.6
  10.9 1.2 copy-start.1
  13.8 0.9 copy-start
  43.4 15.8 %copy-start.10 = (bf16[256,384]{1,0:T(8,128)(2,1)S(1)}, bf16[256,384]{1,0:T(8,128)(2,1)}, u32[]{:S(2)}) copy-start(bf16[256,384]{1,0:T(8,128)(2,1)} %get-tuple-element.58.x_ref) | copy-start | bytes 589828
  50.8 8.4 %collective-permute-start = (bf16[256,384]{1,0:T(8,128)(2,1)}, bf16[256,384]{1,0:T(8,128)(2,1)S(1)}, u32[]{:S(2)}, u32[]{:S(2)}) collective-permute-start(bf16[256,384]{1,0:T(8,128)(2,1)} %get-tuple-element.62), channel_id=1, source_target_pairs={{0,16},{1,17},{2,18},{3,19},{4,20},{5,21},{6,22},{7,23},{8,24},{9,... | collective-permute-start | bytes 589832 | tf_op jit(solution)/shard_map/ppermute | solution.py:641
  59.9 20.3 %copy-start.9 = (bf16[256,384]{1,0:T(8,128)(2,1)S(1)}, bf16[256,384]{1,0:T(8,128)(2,1)}, u32[]{:S(2)}) copy-start(bf16[256,384]{1,0:T(8,128)(2,1)} %get-tuple-element.63.g_ref) | copy-start | bytes 589828
  71.7 8.5 %collective-permute-start.1 = (bf16[256,384]{1,0:T(8,128)(2,1)}, bf16[256,384]{1,0:T(8,128)(2,1)S(1)}, u32[]{:S(2)}, u32[]{:S(2)}) collective-permute-start(bf16[256,384]{1,0:T(8,128)(2,1)} %get-tuple-element.68), channel_id=1, source_target_pairs={{16,0},{17,1},{18,2},{19,3},{20,4},{21,5},{22,6},{23,7},{24,8},{25... | collective-permute-start | bytes 589832 | tf_op jit(solution)/shard_map/ppermute | solution.py:648
  147.2 7.4 %copy-start.4 = (f32[192,576]{1,0:T(8,128)S(1)}, f32[192,576]{1,0:T(8,128)}, u32[]{:S(2)}) copy-start(f32[192,576]{1,0:T(8,128)} %get-tuple-element.96) | copy-start | bytes 1327108
  151.2 4.6 %copy-start.2 = (f32[768,192]{1,0:T(8,128)S(1)}, f32[768,192]{1,0:T(8,128)}, u32[]{:S(2)}) copy-start(f32[768,192]{1,0:T(8,128)} %get-tuple-element.100) | copy-start | bytes 1769476
  168.7 3.2 %copy-start.13 = (f32[2,384]{1,0:T(2,128)S(1)}, f32[2,384]{1,0:T(2,128)}, u32[]{:S(2)}) copy-start(f32[2,384]{1,0:T(2,128)} %get-tuple-element.168) | copy-start | bytes 9220
  168.7 3.7 %copy-start.8 = (f32[192,192]{1,0:T(8,128)S(1)}, f32[192,192]{1,0:T(8,128)}, u32[]{:S(2)}) copy-start(f32[192,192]{1,0:T(8,128)} %get-tuple-element.98) | copy-start | bytes 442372
  168.7 4.4 %copy-start.3 = (f32[192,768]{1,0:T(8,128)S(1)}, f32[192,768]{1,0:T(8,128)}, u32[]{:S(2)}) copy-start(f32[192,768]{1,0:T(8,128)} %get-tuple-element.99) | copy-start | bytes 1769476
